TPU v7x, 32 devices: a whole 2x2x4 slice. The times are simulated.
32 devices in a mesh: tile: 8 (over y, x, core), depth: 4 (over z).
Axes of the slice: x: 2, y: 2, z: 4, core: 2. Of those that a mesh axis runs over, the one named last changes fastest.
Arguments:
- features: bfloat16 [4, 2048, 128], P('depth', 'tile'), may hold values from -4 to 4
- logits: float32 [4, 2048], P('depth', 'tile'), may hold values from -2.75 to 5.5
- geometry: float32 [2, 4, 5, 2048], P(None, 'depth', None, 'tile'), may hold values from -0.6 to 32, as said below
- dest_slot: int32 [2, 4, 2048], P(None, 'depth', 'tile'), may hold values from -1 to 2047, as said below
- target: bfloat16 [2, 16, 128, 1024], P(None, 'tile'), may hold values from -3 to 3
Outputs:
- images: bfloat16 [2, 16, 128, 1024], P(None, 'tile', None, 'depth')
- new_features: bfloat16 [4, 2048, 128], P('depth', 'tile')
- new_logits: float32 [4, 2048], P('depth', 'tile')
- shape_grads: float32 [2, 4, 5, 2048], P(None, 'depth', None, 'tile')
Inputs may be any that keep to these rules, and one draw needn't show every extreme that they name: `dest_slot`: for each view and layer no two splats share a slot; -1 marks a splat outside the view; a splat's place within its tile is its front-to-back order. At most 32 splats of one layer held by one index of tile go to the tiles of one index of tile, and in every view and layer there is an index of tile whose tiles receive exactly 32 from every owner, so that all their slots are used. `geometry`: components 0 and 1 are a splat's centre in pixels within its tile, from 0 to 32; components 2 and 3 lie in -0.5 to 2.0; component 4 in -0.6 to 0.6.
All inputs are finite; a program needn't handle non-finite values.
Results may differ from a plain program's by a relative error of at most 0.0073.
Values may be sent and summed in bfloat16 or wider, within the bound.
A program may use at most 64 MiB of HBM per device.

v0:
```python
from functools import partial

import jax
import jax.numpy as jnp
from jax import lax
from jax.sharding import PartitionSpec as P

F = 128
W = 32
S = 128
VIEWS = 2
P_SIZE = 1024


clamp_top = 0.99
feature_rate = 0.5
opacity_rate = 0.5


def pixel_places():
    places = jnp.arange(P_SIZE, dtype=jnp.int32)
    across = (places % W).astype(jnp.float32) + 0.5
    downward = (places // W).astype(jnp.float32) + 0.5
    return (across, downward)


def block_sum(values, reverse):
    length = values.shape[0]
    block_rows = min(128, length)
    blocks = values.reshape(length // block_rows, block_rows, values.shape[1])
    positions = jnp.arange(block_rows)
    if reverse:
        triangle = (positions[:, None] < positions[None, :]).astype(jnp.float32)
    else:
        triangle = (positions[:, None] > positions[None, :]).astype(jnp.float32)
    within = jnp.einsum("ij,bjp->bip", triangle, blocks, precision=lax.Precision.HIGHEST)
    block_totals = jnp.sum(blocks, axis=1)
    if reverse:
        offsets = jnp.sum(block_totals, axis=0)[None, :] - jnp.cumsum(block_totals, axis=0)
    else:
        offsets = jnp.cumsum(block_totals, axis=0) - block_totals
    return (within + offsets[:, None, :]).reshape(length, values.shape[1])


def splat_fields(shapes):
    across, downward = pixel_places()
    delta_x = across[None, :] - shapes[0][:, None]
    delta_y = downward[None, :] - shapes[1][:, None]
    coef_a = jnp.exp(shapes[2])[:, None]
    coef_c = jnp.exp(shapes[3])[:, None]
    spread = jnp.exp(0.5 * (shapes[2] + shapes[3]))[:, None]
    coef_b = shapes[4][:, None] * spread
    quadric = (
        coef_a * delta_x * delta_x + 2.0 * coef_b * delta_x * delta_y + coef_c * delta_y * delta_y
    )
    falloff = jnp.exp(-0.5 * quadric)
    opacity = shapes[5][:, None]
    product = opacity * falloff
    coverage = jnp.minimum(product, clamp_top)
    return (delta_x, delta_y, coef_a, coef_b, coef_c, spread, falloff, opacity, product, coverage)


def layer_forward(inputs):
    slot_feats, shapes = inputs
    coverage = splat_fields(shapes)[9]
    log_keep = jnp.log(1.0 - coverage)
    before = block_sum(log_keep, False)
    weights = (coverage * jnp.exp(before)).astype(jnp.bfloat16)
    composite = lax.dot_general(
        slot_feats, weights, (((0,), (0,)), ((), ())), preferred_element_type=jnp.float32
    )
    layer_keep = jnp.exp(jnp.sum(log_keep, axis=0))
    return (composite, layer_keep)


def layer_backward(inputs):
    slot_feats, shapes, grad_comp, grad_keep = inputs
    delta_x, delta_y, coef_a, coef_b, coef_c, spread, falloff, opacity, product, coverage = (
        splat_fields(shapes)
    )
    log_keep = jnp.log(1.0 - coverage)
    before = block_sum(log_keep, False)
    decayed = jnp.exp(before)
    exact_weight = coverage * decayed
    weights = exact_weight.astype(jnp.bfloat16)
    layer_keep = jnp.exp(jnp.sum(log_keep, axis=0))
    grad_feat = lax.dot_general(
        weights, grad_comp, (((1,), (1,)), ((), ())), preferred_element_type=jnp.float32
    )
    grad_weight = jnp.dot(slot_feats, grad_comp, preferred_element_type=jnp.float32)
    grad_before = grad_weight * exact_weight
    later = block_sum(grad_before, True)
    grad_log = later + (grad_keep * layer_keep)[None, :]
    grad_coverage = grad_weight * decayed - grad_log / (1.0 - coverage)
    grad_product = jnp.where(product < clamp_top, grad_coverage, 0.0)
    grad_quadric = -0.5 * opacity * falloff * grad_product
    grad_mean_x = -2.0 * jnp.sum(grad_quadric * (coef_a * delta_x + coef_b * delta_y), axis=1)
    grad_mean_y = -2.0 * jnp.sum(grad_quadric * (coef_b * delta_x + coef_c * delta_y), axis=1)
    grad_first = jnp.sum(grad_quadric * delta_x * delta_x, axis=1)
    grad_cross = jnp.sum(grad_quadric * 2.0 * delta_x * delta_y, axis=1)
    grad_second = jnp.sum(grad_quadric * delta_y * delta_y, axis=1)
    grad_log_a = coef_a[:, 0] * grad_first + 0.5 * coef_b[:, 0] * grad_cross
    grad_log_c = coef_c[:, 0] * grad_second + 0.5 * coef_b[:, 0] * grad_cross
    grad_corr = spread[:, 0] * grad_cross
    opacity_flat = opacity[:, 0]
    grad_logit = opacity_flat * (1.0 - opacity_flat) * jnp.sum(falloff * grad_product, axis=1)
    grad_shape = jnp.stack(
        [grad_mean_x, grad_mean_y, grad_log_a, grad_log_c, grad_corr, grad_logit]
    )
    return (grad_feat, grad_shape)


def rear_step(all_keeps, all_terms, depth_here, layers, counter, carried):
    layer_at = layers - 1 - counter
    updated = all_terms[layer_at] + all_keeps[layer_at] * carried
    return jnp.where(layer_at > depth_here, updated, carried)


def body(features, logits, geometry, dest_slot, target):
    owners = lax.axis_size("tile")
    layers = lax.axis_size("depth")
    depth_here = lax.axis_index("depth")
    tiles_here = target.shape[1]
    owned = features.shape[1]
    capacity = owned // owners
    pixel_share = P_SIZE // layers
    splat_feats = features[0]
    logit_now = logits[0]
    images = []
    shape_grads = []
    for view_index in range(VIEWS):
        slot_ids = dest_slot[view_index, 0]
        visible = slot_ids >= 0
        receiver = jnp.where(visible, slot_ids // owned, owners)
        matches = (receiver[:, None] == jnp.arange(owners, dtype=jnp.int32)[None, :]).astype(
            jnp.int32
        )
        place_in = jnp.sum((jnp.cumsum(matches, axis=0) - matches) * matches, axis=1)
        position = jnp.where(visible, receiver * capacity + place_in, owners * capacity)
        local_slot = jnp.where(visible, slot_ids - receiver * owned, -1)
        opacity = jax.nn.sigmoid(logit_now)
        shape_rows = jnp.concatenate([geometry[view_index, 0], opacity[None, :]], axis=0).T
        row_buffer = (
            jnp.zeros((owners * capacity + 1, F), jnp.bfloat16)
            .at[position]
            .set(splat_feats)[:-1]
            .reshape(owners, capacity, F)
        )
        slot_buffer = (
            jnp.full((owners * capacity + 1,), -1, jnp.int32)
            .at[position]
            .set(local_slot)[:-1]
            .reshape(owners, capacity)
        )
        shape_buffer = (
            jnp.zeros((owners * capacity + 1, 6), jnp.float32)
            .at[position]
            .set(shape_rows)[:-1]
            .reshape(owners, capacity, 6)
        )
        got_rows, got_slots = (
            lax.all_to_all(row_buffer, "tile", split_axis=0, concat_axis=0, tiled=True),
            lax.all_to_all(slot_buffer, "tile", split_axis=0, concat_axis=0, tiled=True),
        )
        got_shapes = lax.all_to_all(shape_buffer, "tile", split_axis=0, concat_axis=0, tiled=True)
        arrived = got_slots.reshape(-1)
        present = arrived >= 0
        landing = jnp.where(present, arrived, owned)
        slot_feats = (
            jnp.zeros((owned + 1, F), jnp.bfloat16)
            .at[landing]
            .set(got_rows.reshape(-1, F))[:-1]
            .reshape(tiles_here, S, F)
        )
        slot_shapes = (
            jnp.zeros((owned + 1, 6), jnp.float32)
            .at[landing]
            .set(got_shapes.reshape(-1, 6))[:-1]
            .reshape(tiles_here, S, 6)
            .transpose(0, 2, 1)
        )
        composites, layer_keeps = lax.map(layer_forward, (slot_feats, slot_shapes))
        all_keeps = lax.all_gather(layer_keeps[None], "depth", axis=0, tiled=True)
        earlier_mask = (jnp.arange(layers) < depth_here)[:, None, None]
        ahead = jnp.prod(jnp.where(earlier_mask, all_keeps, 1.0), axis=0)
        contrib = ahead[:, None, :] * composites
        summed = lax.psum(contrib, "depth")
        residual = summed - target[view_index].astype(jnp.float32)
        image_part = lax.dynamic_slice_in_dim(summed, depth_here * pixel_share, pixel_share, 2)
        images.append(image_part.astype(jnp.bfloat16))
        pixel_terms = jnp.sum(residual * composites, axis=1)
        all_terms = lax.all_gather(pixel_terms[None], "depth", axis=0, tiled=True)
        behind = lax.fori_loop(
            0,
            layers,
            partial(rear_step, all_keeps, all_terms, depth_here, layers),
            jnp.zeros_like(pixel_terms),
        )
        grad_keep = ahead * behind
        grad_comp = (ahead[:, None, :] * residual).astype(jnp.bfloat16)
        grad_feat, grad_shape = lax.map(
            layer_backward, (slot_feats, slot_shapes, grad_comp, grad_keep)
        )
        flat_feat = grad_feat.reshape(owned, F)
        flat_shape = grad_shape.transpose(0, 2, 1).reshape(owned, 6)
        fetched = jnp.where(present, arrived, 0)
        back_feat = jnp.where(present[:, None], flat_feat[fetched], 0.0).reshape(
            owners, capacity, F
        )
        back_shape = jnp.where(present[:, None], flat_shape[fetched], 0.0).reshape(
            owners, capacity, 6
        )
        return_feat, return_shape = (
            lax.all_to_all(back_feat, "tile", split_axis=0, concat_axis=0, tiled=True),
            lax.all_to_all(back_shape, "tile", split_axis=0, concat_axis=0, tiled=True),
        )
        padded_feat = jnp.concatenate(
            [return_feat.reshape(-1, F), jnp.zeros((1, F), jnp.float32)], axis=0
        )
        padded_shape = jnp.concatenate(
            [return_shape.reshape(-1, 6), jnp.zeros((1, 6), jnp.float32)], axis=0
        )
        splat_grad_feat = padded_feat[position]
        splat_grad_shape = padded_shape[position]
        shape_grads.append(splat_grad_shape[:, :5].T)
        splat_feats = (splat_feats.astype(jnp.float32) - feature_rate * splat_grad_feat).astype(
            jnp.bfloat16
        )
        logit_now = logit_now - opacity_rate * splat_grad_shape[:, 5]
    return (jnp.stack(images), splat_feats[None], logit_now[None], jnp.stack(shape_grads)[:, None])


def solution(mesh):
    placed = (
        P("depth", "tile", None),
        P("depth", "tile"),
        P(None, "depth", None, "tile"),
        P(None, "depth", "tile"),
        P(None, "tile", None, None),
    )
    return jax.shard_map(
        body,
        mesh=mesh,
        in_specs=placed,
        out_specs=(
            P(None, "tile", None, "depth"),
            P("depth", "tile", None),
            P("depth", "tile"),
            P(None, "depth", None, "tile"),
        ),
        check_vma=False,
    )
```

profile of v0, /device:TPU:0, one launch (start us, length us, event | category | flops | bytes accessed | tf_op | source)
XLA Modules:
  0.0 308.5 jit_solution(4619955164635074478)
XLA Ops:
  13.0 1.4 scatter_custom_fusion
  15.1 5.3 %all-to-all-start = ((s32[8,1,32]{2,1,0:T(1,128)}), s32[8,1,32]{2,1,0:T(1,128)S(1)}, u32[]{:S(2)}, u32[]{:S(2)}) async-start(s32[8,1,32]{2,1,0:T(1,128)} %all_to_all.36), calls=%async_computation | async-start | bytes 8192 | tf_op jit(solution)/shard_map/all_to_all | solution.py:163
  20.7 1.2 scatter_custom_fusion.3
  22.7 2.4 all-to-all-done
  25.1 3.3 %all-to-all-start.2 = ((f32[8,1,192]{2,1,0:T(1,128)}), f32[8,1,192]{2,1,0:T(1,128)S(1)}, u32[]{:S(2)}, u32[]{:S(2)}) async-start(f32[8,1,192]{2,1,0:T(1,128)} %reshape.3803), calls=%async_computation.2 | async-start | bytes 16384 | tf_op jit(solution)/shard_map/all_to_all | solution.py:165
  28.4 1.2 scatter_custom_fusion.1
  31.5 1.6 all-to-all-done.2
  33.1 3.4 %all-to-all-start.1 = ((bf16[8,32,128]{2,1,0:T(8,128)(2,1)}), bf16[8,32,128]{2,1,0:T(8,128)(2,1)S(1)}, u32[]{:S(2)}, u32[]{:S(2)}) async-start(bf16[8,32,128]{2,1,0:T(8,128)(2,1)} %bitcast.95), calls=%async_computation.1 | async-start | bytes 131072 | tf_op jit(solution)/shard_map/all_to_all | solution.py:162
  39.0 2.4 all-to-all-done.1
  41.4 1.2 scatter_custom_fusion.2
  44.0 5.1 %while.88 = (s32[]{:T(128)}, f32[2,128,1024]{2,1,0:T(8,128)S(1)}, f32[2,1024]{1,0:T(2,128)S(1)}, bf16[2,128,128]{2,1,0:T(8,128)(2,1)S(1)}, f32[2,6,128]{2,1,0:T(8,128)S(1)}, /*index=5*/s32[]{:T(128)}, s32[]{:T(128)}) while((s32[]{:T(128)}, f32[2,128,1024]{2,1,0:T(8,128)S(1)}, f32[2,1024]{1,0:T(2,128)S(1)}, ...), condition=%wide.region_11.12_spmd, body=%wide.region_8.11_spmd.sunk | while | flops 242777600 | bytes 1177693 | solution.py:182
  45.1 1.2 fusion.315
  47.6 1.2 fusion.315
  49.1 13.4 %all-gather.4 = f32[4,2,1024]{2,1,0:T(2,128)S(1)} all-gather(f32[1,2,1024]{2,1,0:T(2,128)S(1)} %bitcast.689), channel_id=2, replica_groups=mesh['tile'=8,'depth'=4] {'depth'}, dimensions={0}, use_global_device_ids=true | all-gather | bytes 40960 | tf_op jit(solution)/shard_map/all_gather | solution.py:183
  63.8 1.4 scatter_custom_fusion.5
  65.9 49.1 %all-reduce.7.cloned.1.call-done = f32[2,128,1024]{2,1,0:T(8,128)} async-done(((f32[2,128,1024]{2,1,0:T(8,128)}), f32[2,128,1024]{2,1,0:T(8,128)}) %all-reduce.7.cloned.1.call-update) | async-done | bytes 1048592 | tf_op jit(solution)/shard_map/psum | solution.py:187
  115.0 1.5 multiply_reduce_fusion.3
  116.5 13.3 %all-gather.5 = f32[4,2,1024]{2,1,0:T(2,128)S(1)} all-gather(f32[1,2,1024]{2,1,0:T(2,128)S(1)} %bitcast.687), channel_id=3, replica_groups=mesh['tile'=8,'depth'=4] {'depth'}, dimensions={0}, use_global_device_ids=true | all-gather | bytes 40960 | tf_op jit(solution)/shard_map/all_gather | solution.py:192
  130.0 9.6 %while.89 = (s32[]{:T(128)}, f32[2,128,128]{2,1,0:T(8,128)S(1)}, f32[2,6,128]{2,1,0:T(8,128)S(1)}, f32[2,6,128]{2,1,0:T(8,128)S(1)}, bf16[2,128,1024]{2,1,0:T(8,...) while((s32[]{:T(128)}, f32[2,128,128]{2,1,0:T(8,128)S(1)}, ...), condition=%wide.region_31.32_spmd, body=%wide.region_21.31_spmd.sunk | while | flops 485672448 | bytes 3947113 | solution.py:201
  132.9 1.9 fusion.325
  137.7 1.9 fusion.325
  142.1 3.7 %all-to-all-start.6 = ((f32[8,1,192]{2,1,0:T(1,128)}), f32[8,1,192]{2,1,0:T(1,128)S(1)}, u32[]{:S(2)}, u32[]{:S(2)}) async-start(f32[8,1,192]{2,1,0:T(1,128)} %reshape.3805), calls=%async_computation.6 | async-start | bytes 16384 | tf_op jit(solution)/shard_map/all_to_all | solution.py:215
  146.5 4.0 %all-to-all-done.6 = f32[8,1,192]{2,1,0:T(1,128)S(1)} async-done(((f32[8,1,192]{2,1,0:T(1,128)}), f32[8,1,192]{2,1,0:T(1,128)S(1)}, u32[]{:S(2)}, u32[]{:S(2)}) %all-to-all-start.6) | async-done | bytes 6176 | tf_op jit(solution)/shard_map/all_to_all | solution.py:215
  150.4 3.3 %all-to-all-start.3 = ((s32[8,1,32]{2,1,0:T(1,128)}), s32[8,1,32]{2,1,0:T(1,128)S(1)}, u32[]{:S(2)}, u32[]{:S(2)}) async-start(s32[8,1,32]{2,1,0:T(1,128)} %all_to_all.40), calls=%async_computation.3 | async-start | bytes 8192 | tf_op jit(solution)/shard_map/all_to_all | solution.py:163
  155.5 2.8 all-to-all-done.3
  158.3 3.4 %all-to-all-start.4 = ((f32[8,32,128]{2,1,0:T(8,128)}), f32[8,32,128]{2,1,0:T(8,128)S(1)}, u32[]{:S(2)}, u32[]{:S(2)}) async-start(f32[8,32,128]{2,1,0:T(8,128)} %broadcast_select_fusion.1), calls=%async_computation.4 | async-start | bytes 262144 | tf_op jit(solution)/shard_map/all_to_all | solution.py:214
  161.9 1.2 scatter_custom_fusion.8
  163.9 3.3 %all-to-all-done.4 = f32[8,32,128]{2,1,0:T(8,128)S(1)} async-done(((f32[8,32,128]{2,1,0:T(8,128)}), f32[8,32,128]{2,1,0:T(8,128)S(1)}, u32[]{:S(2)}, u32[]{:S(2)}) %all-to-all-start.4) | async-done | bytes 131104 | tf_op jit(solution)/shard_map/all_to_all | solution.py:214
  167.1 3.3 %all-to-all-start.7 = ((f32[8,1,192]{2,1,0:T(1,128)}), f32[8,1,192]{2,1,0:T(1,128)S(1)}, u32[]{:S(2)}, u32[]{:S(2)}) async-start(f32[8,1,192]{2,1,0:T(1,128)} %reshape.3807), calls=%async_computation.7 | async-start | bytes 16384 | tf_op jit(solution)/shard_map/all_to_all | solution.py:165
  171.9 1.2 scatter_custom_fusion.6
  173.8 1.3 all-to-all-done.7
  175.1 3.4 %all-to-all-start.5 = ((bf16[8,32,128]{2,1,0:T(8,128)(2,1)}), bf16[8,32,128]{2,1,0:T(8,128)(2,1)S(1)}, u32[]{:S(2)}, u32[]{:S(2)}) async-start(bf16[8,32,128]{2,1,0:T(8,128)(2,1)} %bitcast.121), calls=%async_computation.5 | async-start | bytes 131072 | tf_op jit(solution)/shard_map/all_to_all | solution.py:162
  180.6 2.9 all-to-all-done.5
  183.4 1.2 scatter_custom_fusion.7
  186.1 5.1 %while.90 = (s32[]{:T(128)}, f32[2,128,1024]{2,1,0:T(8,128)S(1)}, f32[2,1024]{1,0:T(2,128)S(1)}, bf16[2,128,128]{2,1,0:T(8,128)(2,1)S(1)}, f32[2,6,128]{2,1,0:T(8,128)S(1)}, /*index=5*/s32[]{:T(128)}, s32[]{:T(128)}) while((s32[]{:T(128)}, f32[2,128,1024]{2,1,0:T(8,128)S(1)}, f32[2,1024]{1,0:T(2,128)S(1)}, ...), condition=%wide.region_39.40_spmd, body=%wide.region_36.39_spmd.sunk | while | flops 242777600 | bytes 1177693 | solution.py:182
  187.1 1.2 fusion.331
  189.7 1.2 fusion.331
  191.2 13.1 %all-gather.6 = f32[4,2,1024]{2,1,0:T(2,128)S(1)} all-gather(f32[1,2,1024]{2,1,0:T(2,128)S(1)} %bitcast.691), channel_id=4, replica_groups=mesh['tile'=8,'depth'=4] {'depth'}, dimensions={0}, use_global_device_ids=true | all-gather | bytes 40960 | tf_op jit(solution)/shard_map/all_gather | solution.py:183
  206.7 48.4 %all-reduce.9.cloned.1.call-done = f32[2,128,1024]{2,1,0:T(8,128)} async-done(((f32[2,128,1024]{2,1,0:T(8,128)}), f32[2,128,1024]{2,1,0:T(8,128)}) %all-reduce.9.cloned.1.call-update) | async-done | bytes 1048592 | tf_op jit(solution)/shard_map/psum | solution.py:187
  255.1 1.5 multiply_reduce_fusion.2
  256.6 13.4 %all-gather.7 = f32[4,2,1024]{2,1,0:T(2,128)S(1)} all-gather(f32[1,2,1024]{2,1,0:T(2,128)S(1)} %bitcast.688), channel_id=5, replica_groups=mesh['tile'=8,'depth'=4] {'depth'}, dimensions={0}, use_global_device_ids=true | all-gather | bytes 40960 | tf_op jit(solution)/shard_map/all_gather | solution.py:192
  270.2 9.7 %while.91 = (s32[]{:T(128)}, f32[2,128,128]{2,1,0:T(8,128)S(1)}, f32[2,6,128]{2,1,0:T(8,128)S(1)}, f32[2,6,128]{2,1,0:T(8,128)S(1)}, bf16[2,128,1024]{2,1,0:T(8,...) while((s32[]{:T(128)}, f32[2,128,128]{2,1,0:T(8,128)S(1)}, ...), condition=%wide.region_55.56_spmd, body=%wide.region_45.55_spmd.sunk | while | flops 485672448 | bytes 3947113 | solution.py:201
  273.0 1.9 fusion.341
  277.9 1.9 fusion.341
  283.0 3.7 %all-to-all-start.9 = ((f32[8,1,192]{2,1,0:T(1,128)}), f32[8,1,192]{2,1,0:T(1,128)S(1)}, u32[]{:S(2)}, u32[]{:S(2)}) async-start(f32[8,1,192]{2,1,0:T(1,128)} %reshape.3809), calls=%async_computation.9 | async-start | bytes 16384 | tf_op jit(solution)/shard_map/all_to_all | solution.py:215
  288.4 3.0 all-to-all-done.9
  291.4 3.4 %all-to-all-start.8 = ((f32[8,32,128]{2,1,0:T(8,128)}), f32[8,32,128]{2,1,0:T(8,128)S(1)}, u32[]{:S(2)}, u32[]{:S(2)}) async-start(f32[8,32,128]{2,1,0:T(8,128)} %broadcast_select_fusion), calls=%async_computation.8 | async-start | bytes 262144 | tf_op jit(solution)/shard_map/all_to_all | solution.py:214
  297.8 2.4 all-to-all-done.8
  (264 shorter events, 55.0 us)
Async XLA Ops:
  8.8 0.6 copy-start.6
  10.2 0.6 copy-start.7
  10.8 0.7 slice-start.2
  11.5 0.7 slice-start.3
  12.3 0.7 copy-start.5
  13.0 7.5 %copy-start.4 = (f32[2,1,5,256]{3,1,2,0:T(1,128)S(1)}, f32[2,1,5,256]{3,1,2,0:T(1,128)}, u32[]{:S(2)}) copy-start(f32[2,1,5,256]{3,1,2,0:T(1,128)} %param.19) | copy-start | bytes 30724
  15.1 5.3 %copy-start.8 = (f32[1,256]{1,0:T(1,128)S(1)}, f32[1,256]{1,0:T(1,128)}, u32[]{:S(2)}) copy-start(f32[1,256]{1,0:T(1,128)} %param.18) | copy-start | bytes 3076
  15.1 9.9 %all-to-all-start = ((s32[8,1,32]{2,1,0:T(1,128)}), s32[8,1,32]{2,1,0:T(1,128)S(1)}, u32[]{:S(2)}, u32[]{:S(2)}) async-start(s32[8,1,32]{2,1,0:T(1,128)} %all_to_all.36), calls=%async_computation | async-start | bytes 8192 | tf_op jit(solution)/shard_map/all_to_all | solution.py:163
  21.9 6.6 %copy-start.3 = (bf16[1,256,128]{2,1,0:T(8,128)(2,1)S(1)}, bf16[1,256,128]{2,1,0:T(8,128)(2,1)}, u32[]{:S(2)}) copy-start(bf16[1,256,128]{2,1,0:T(8,128)(2,1)} %param.17) | copy-start | bytes 196612
  25.1 8.0 %all-to-all-start.2 = ((f32[8,1,192]{2,1,0:T(1,128)}), f32[8,1,192]{2,1,0:T(1,128)S(1)}, u32[]{:S(2)}, u32[]{:S(2)}) async-start(f32[8,1,192]{2,1,0:T(1,128)} %reshape.3803), calls=%async_computation.2 | async-start | bytes 16384 | tf_op jit(solution)/shard_map/all_to_all | solution.py:165
  33.1 8.3 %all-to-all-start.1 = ((bf16[8,32,128]{2,1,0:T(8,128)(2,1)}), bf16[8,32,128]{2,1,0:T(8,128)(2,1)S(1)}, u32[]{:S(2)}, u32[]{:S(2)}) async-start(bf16[8,32,128]{2,1,0:T(8,128)(2,1)} %bitcast.95), calls=%async_computation.1 | async-start | bytes 131072 | tf_op jit(solution)/shard_map/all_to_all | solution.py:162
  36.4 78.5 %all-reduce.7.cloned.1.call-start = ((), (), s32[]{:S(2)}) async-start(), calls=%async_computation.10 | async-start | bytes 2097152 | tf_op jit(solution)/shard_map/psum | solution.py:187
  42.6 0.6 copy-start.2
  43.2 0.8 slice-start.1
  63.8 51.2 %copy-start = (bf16[2,2,128,1024]{3,2,1,0:T(8,128)(2,1)S(1)}, bf16[2,2,128,1024]{3,2,1,0:T(8,128)(2,1)}, u32[]{:S(2)}) copy-start(bf16[2,2,128,1024]{3,2,1,0:T(8,128)(2,1)} %param.21) | copy-start | bytes 3145732
  142.1 8.4 %all-to-all-start.6 = ((f32[8,1,192]{2,1,0:T(1,128)}), f32[8,1,192]{2,1,0:T(1,128)S(1)}, u32[]{:S(2)}, u32[]{:S(2)}) async-start(f32[8,1,192]{2,1,0:T(1,128)} %reshape.3805), calls=%async_computation.6 | async-start | bytes 16384 | tf_op jit(solution)/shard_map/all_to_all | solution.py:215
  150.4 7.9 %all-to-all-start.3 = ((s32[8,1,32]{2,1,0:T(1,128)}), s32[8,1,32]{2,1,0:T(1,128)S(1)}, u32[]{:S(2)}, u32[]{:S(2)}) async-start(s32[8,1,32]{2,1,0:T(1,128)} %all_to_all.40), calls=%async_computation.3 | async-start | bytes 8192 | tf_op jit(solution)/shard_map/all_to_all | solution.py:163
  158.3 8.8 %all-to-all-start.4 = ((f32[8,32,128]{2,1,0:T(8,128)}), f32[8,32,128]{2,1,0:T(8,128)S(1)}, u32[]{:S(2)}, u32[]{:S(2)}) async-start(f32[8,32,128]{2,1,0:T(8,128)} %broadcast_select_fusion.1), calls=%async_computation.4 | async-start | bytes 262144 | tf_op jit(solution)/shard_map/all_to_all | solution.py:214
  167.1 8.0 %all-to-all-start.7 = ((f32[8,1,192]{2,1,0:T(1,128)}), f32[8,1,192]{2,1,0:T(1,128)S(1)}, u32[]{:S(2)}, u32[]{:S(2)}) async-start(f32[8,1,192]{2,1,0:T(1,128)} %reshape.3807), calls=%async_computation.7 | async-start | bytes 16384 | tf_op jit(solution)/shard_map/all_to_all | solution.py:165
  175.1 8.3 %all-to-all-start.5 = ((bf16[8,32,128]{2,1,0:T(8,128)(2,1)}), bf16[8,32,128]{2,1,0:T(8,128)(2,1)S(1)}, u32[]{:S(2)}, u32[]{:S(2)}) async-start(bf16[8,32,128]{2,1,0:T(8,128)(2,1)} %bitcast.121), calls=%async_computation.5 | async-start | bytes 131072 | tf_op jit(solution)/shard_map/all_to_all | solution.py:162
  178.5 76.6 %all-reduce.9.cloned.1.call-start = ((), (), s32[]{:S(2)}) async-start(), calls=%async_computation.11 | async-start | bytes 2097152 | tf_op jit(solution)/shard_map/psum | solution.py:187
  184.6 0.6 copy-start.1
  185.2 0.8 slice-start
  283.0 8.4 %all-to-all-start.9 = ((f32[8,1,192]{2,1,0:T(1,128)}), f32[8,1,192]{2,1,0:T(1,128)S(1)}, u32[]{:S(2)}, u32[]{:S(2)}) async-start(f32[8,1,192]{2,1,0:T(1,128)} %reshape.3809), calls=%async_computation.9 | async-start | bytes 16384 | tf_op jit(solution)/shard_map/all_to_all | solution.py:215
  291.4 8.8 %all-to-all-start.8 = ((f32[8,32,128]{2,1,0:T(8,128)}), f32[8,32,128]{2,1,0:T(8,128)S(1)}, u32[]{:S(2)}, u32[]{:S(2)}) async-start(f32[8,32,128]{2,1,0:T(8,128)} %broadcast_select_fusion), calls=%async_computation.8 | async-start | bytes 262144 | tf_op jit(solution)/shard_map/all_to_all | solution.py:214
Sparse Core Ops, SparseCore 0:
  63.9 51.0 all-reduce.6
  205.7 49.3 all-reduce.8
where the time goes:
time: 310 us; the launch traced here: 308 us
  waiting for transfers between devices  123 us (40%)
  blocking collectives  53.2 us (17%)
  starting transfers between devices  36.2 us (12%)
  local copies, waits for them, and re-layouts  35.9 us (12%)
  matrix products  22.2 us (7%)
  other arithmetic  21.8 us (7%)
  between operations  14.7 us (5%)
    psum x2, waiting for transfers between devices, body(): summed = lax.psum(contrib, 'depth')  97.4 us
    all_gather x2, blocking collectives, body(): all_terms = lax.all_gather(pixel_terms[None], 'depth', axis=0, tiled=True)  26.7 us
    all_gather x2, blocking collectives, body(): all_keeps = lax.all_gather(layer_keeps[None], 'depth', axis=0, tiled=True)  26.5 us
    dot_general x12, matrix products, block_sum(): jnp.einsum('ij,bjp->bip', triangle, blocks, precision=lax.Precision.HIGHEST)  15.4 us
    all_to_all x2, starting transfers between devices, body(): lax.all_to_all(slot_buffer, 'tile', split_axis=0, concat_axis=0, tiled=True)  8.64 us
    all_to_all x2, starting transfers between devices, body(): lax.all_to_all(back_shape, 'tile', split_axis=0, concat_axis=0, tiled=True)  7.31 us
    all_to_all x2, waiting for transfers between devices, body(): lax.all_to_all(back_shape, 'tile', split_axis=0, concat_axis=0, tiled=True)  6.97 us
    unnamed x28, local copies, waits for them, and re-layouts  6.8 us
  transfers between devices with their start and end apart: 12, of which 12 were waited for; matrix products, arithmetic and copies ran while one was open for 8% of the time, Pallas kernels for 0%

commit v1 on v0

v1 whole, which is shorter than its diff:
```python
import functools

import jax
import jax.numpy as jnp
from jax import lax
from jax.experimental import pallas as pl
from jax.experimental.pallas import tpu as pltpu
from jax.sharding import PartitionSpec as P

W = 32
S = 128
clamp_top = 0.99
feature_rate = 0.5
opacity_rate = 0.5
f32 = jnp.float32
bf16 = jnp.bfloat16


def dot(lhs, rhs, left=1, right=0):
    return lax.dot_general(
        lhs, rhs, (((left,), (right,)), ((), ())), preferred_element_type=f32
    )


def three_parts(value):
    high = value.astype(bf16).astype(f32)
    rest = value - high
    mid = rest.astype(bf16).astype(f32)
    return high, mid, rest - mid


def two_parts(value):
    high = value.astype(bf16)
    low = (value - high.astype(f32)).astype(bf16)
    return jnp.concatenate([high, low], axis=1)


def iota(shape, axis):
    return lax.broadcasted_iota(jnp.int32, shape, axis)


def put_rows(rows, shape):
    place = iota(shape, 0)
    total = jnp.zeros(shape, f32)
    for at, row in enumerate(rows):
        total = jnp.where(place == at, row, total)
    return total


def splat_kernel(
    owners, layers, views, tiles, share,
    feat_ref, logit_ref, geom_ref, dest_ref, target_ref,
    img_ref, newf_ref, newl_ref, sg_ref,
    pay, got, back, ret, gath_f, gath_s, part_f, part_s, in_f, in_s,
    perm, place_t, places, tri, tril, ones2,
    fall_s, dec_s, w_s, comp_s, keep_s, ahead_s, gk_s, res_s, run_s,
    cur_f, cur_l,
    a_send, a_recv, gf_send, gf_recv, gs_send, gs_recv,
    pf_send, pf_recv, ps_send, ps_recv, b_send, b_recv,
):
    me_t = lax.axis_index("tile")
    me_d = lax.axis_index("depth")
    owned, feats = feat_ref.shape
    cap = owned // owners
    wire = pay.dtype

    def tile_peer(k):
        return lax.rem(me_t + k, owners)

    def depth_peer(k):
        return lax.rem(me_d + k, layers)

    barrier = pltpu.get_barrier_semaphore()
    for k in range(1, owners):
        pl.semaphore_signal(barrier, inc=1, device_id=(tile_peer(k), me_d), device_id_type=pl.DeviceIdType.MESH)
    for k in range(1, layers):
        pl.semaphore_signal(barrier, inc=1, device_id=(me_t, depth_peer(k)), device_id_type=pl.DeviceIdType.MESH)

    pixel = iota((share, S), 0) + me_d * share
    places[0] = (pixel & (W - 1)).astype(f32) + 0.5
    places[1] = (pixel >> (W.bit_length() - 1)).astype(f32) + 0.5
    row = iota((S, S), 0)
    col = iota((S, S), 1)
    earlier = (row < col).astype(f32).astype(bf16)
    later_mat = (row > col).astype(f32).astype(bf16)
    ones = jnp.ones((S, S), bf16)
    half = jnp.concatenate([earlier, ones], axis=1)
    tri[...] = jnp.concatenate([half, half], axis=0)
    tril[...] = jnp.concatenate([later_mat, later_mat], axis=0)
    ones2[...] = jnp.ones((2 * feats, feats), bf16)
    cur_f[...] = feat_ref[...]
    cur_l[...] = logit_ref[...]

    pl.semaphore_wait(barrier, owners + layers - 2)

    def tile_copy(v, k, src, dst, send, recv):
        return pltpu.make_async_remote_copy(
            src_ref=src.at[v, tile_peer(k)], dst_ref=dst.at[v, me_t],
            send_sem=send.at[v, k], recv_sem=recv.at[v, k],
            device_id=(tile_peer(k), me_d), device_id_type=pl.DeviceIdType.MESH,
        )

    def exchange(v, src, dst, send, recv):
        for k in range(1, owners):
            tile_copy(v, k, src, dst, send, recv).start()
        dst[v, me_t] = src[v, me_t]
        for k in range(1, owners):
            tile_copy(v, k, src, dst, send, recv).wait()

    def depth_copy(v, k, src, dst, src_at, send, recv):
        return pltpu.make_async_remote_copy(
            src_ref=src.at[v, src_at], dst_ref=dst.at[v, me_d],
            send_sem=send.at[v, k], recv_sem=recv.at[v, k],
            device_id=(me_t, depth_peer(k)), device_id_type=pl.DeviceIdType.MESH,
        )

    def slot_rows(v, e, t):
        g = gath_s[v, e, :, t * S : (t + 1) * S]
        coef_a = jnp.exp(g[2:3])
        coef_c = jnp.exp(g[3:4])
        spread = jnp.exp(0.5 * (g[2:3] + g[3:4]))
        return g[0:1], g[1:2], coef_a, g[4:5] * spread, coef_c, spread, g[5:6]

    def forward(v, e):
        for t in range(tiles):
            g0, g1, ca, cb, cc, _, opacity = slot_rows(v, e, t)
            dx = places[0] - g0
            dy = places[1] - g1
            quadric = ca * dx * dx + 2.0 * cb * dx * dy + cc * dy * dy
            fall = jnp.exp(-0.5 * quadric)
            coverage = jnp.minimum(opacity * fall, clamp_top)
            log_keep = jnp.log(1.0 - coverage)
            sums = dot(two_parts(log_keep), tri[...])
            decayed = jnp.exp(sums[:, :S])
            weights = (coverage * decayed).astype(bf16)
            fall_s[e, t] = fall
            dec_s[e, t] = decayed
            w_s[e, t] = weights
            keep_s[e, t] = jnp.exp(sums[:, S:])
            comp_s[e, t] = dot(weights, gath_f[v, e, t * S : (t + 1) * S, :])

    def combine(v):
        for t in range(tiles):
            res_s[t] = jnp.zeros((share, feats), f32)
            run_s[...] = jnp.ones((share, feats), f32)

            def front(e, carry):
                ahead = run_s[...]
                ahead_s[e, t] = ahead
                res_s[t] = res_s[t] + ahead * comp_s[e, t]
                run_s[...] = ahead * keep_s[e, t]
                return carry

            lax.fori_loop(0, layers, front, 0)
            summed = res_s[t]
            img_ref[v, t] = summed.astype(bf16)
            res_s[t] = summed - target_ref[v, t].astype(f32)
            run_s[...] = jnp.zeros((share, feats), f32)

            def rear(i, carry):
                e = layers - 1 - i
                behind = run_s[...]
                keep = keep_s[e, t]
                gk_s[e, t] = ahead_s[e, t] * behind * keep
                terms = dot(two_parts(res_s[t] * comp_s[e, t]), ones2[...])
                run_s[...] = terms + keep * behind
                return carry

            lax.fori_loop(0, layers, rear, 0)

    def backward(v, e):
        for t in range(tiles):
            g0, g1, ca, cb, cc, spread, opacity = slot_rows(v, e, t)
            grad_comp = (ahead_s[e, t] * res_s[t]).astype(bf16)
            span = slice(t * S, (t + 1) * S)
            part_f[v, e, span, :] = dot(w_s[e, t], grad_comp, 0, 0).astype(bf16)
            grad_weight = dot(grad_comp, gath_f[v, e, span, :], 1, 1)
            decayed = dec_s[e, t]
            fall = fall_s[e, t]
            product = opacity * fall
            coverage = jnp.minimum(product, clamp_top)
            grad_decayed = grad_weight * decayed
            later = dot(two_parts(grad_decayed * coverage), tril[...])
            grad_log = later + gk_s[e, t]
            grad_coverage = grad_decayed - grad_log / (1.0 - coverage)
            moment = fall * jnp.where(product < clamp_top, grad_coverage, 0.0)
            dx = places[0] - g0
            dy = places[1] - g1
            moment_x = moment * dx
            moment_y = moment * dy

            def total(value):
                return jnp.sum(value, axis=0, keepdims=True)

            m0 = total(moment)
            mx = opacity * total(moment_x)
            my = opacity * total(moment_y)
            first = -0.5 * opacity * total(moment_x * dx)
            cross = -1.0 * opacity * total(moment_x * dy)
            second = -0.5 * opacity * total(moment_y * dy)
            part_s[v, e, :, span] = put_rows(
                [
                    ca * mx + cb * my,
                    cb * mx + cc * my,
                    ca * first + 0.5 * cb * cross,
                    cc * second + 0.5 * cb * cross,
                    spread * cross,
                    opacity * (1.0 - opacity) * m0,
                ],
                (8, S),
            )

    def aux_rows(eight):
        high, mid, low = three_parts(eight)
        zero = jnp.zeros((feats - 24, owned), f32)
        return jnp.concatenate([high, mid, low, zero], axis=0).astype(bf16)

    def pack(ref, v, value):
        ref[v] = value.reshape(owners, cap, value.shape[1]).astype(wire)

    def unpack(ref, v):
        return ref[v].astype(f32).reshape(owners * cap, 2 * feats)

    for v in range(views):
        dest = dest_ref[v]
        low_edge = iota((owners, owned), 0) * owned
        hit = (dest >= low_edge) & (dest < low_edge + owned)
        matches = hit.astype(f32)
        upper = (iota((owned, owned), 0) < iota((owned, owned), 1)).astype(f32).astype(bf16)
        rank = dot(matches.astype(bf16), upper)
        count = iota((owners, owned), 0).astype(f32) * cap + rank + 1.0
        position = jnp.sum(matches * count, axis=0, keepdims=True) - 1.0
        slot_id = jnp.sum(
            matches * (dest - low_edge + 1).astype(f32), axis=0, keepdims=True
        )
        perm_now = (iota((owned, owned), 0).astype(f32) == position).astype(f32).astype(bf16)
        perm[v] = perm_now
        logit = cur_l[...]
        opacity = 1.0 / (1.0 + jnp.exp(-logit))
        rows8 = iota((8, owned), 0)
        eight = jnp.where(rows8 == 5, opacity, jnp.where(rows8 == 6, slot_id, geom_ref[v]))
        pack(
            pay, v,
            jnp.concatenate(
                [dot(perm_now, cur_f[...]), dot(perm_now, aux_rows(eight), 1, 1)], axis=1
            ),
        )
        exchange(v, pay, got, a_send, a_recv)

        arrived = unpack(got, v)
        aux = arrived[:, feats:]
        aux_t = aux.T
        to_slot = (iota((owned, owned), 0).astype(f32) + 1.0 == aux_t[6:7, :]).astype(f32).astype(bf16)
        place_t[v] = (iota((owned, owned), 1).astype(f32) + 1.0 == aux[:, 6:7]).astype(f32).astype(bf16)
        gath_f[v, me_d] = dot(to_slot, arrived[:, :feats].astype(bf16)).astype(bf16)
        shapes = dot(aux_t[0:32].astype(bf16), to_slot, 1, 1)
        gath_s[v, me_d] = shapes[0:8] + shapes[8:16] + shapes[16:24]
        for k in range(1, layers):
            depth_copy(v, k, gath_f, gath_f, me_d, gf_send, gf_recv).start()
            depth_copy(v, k, gath_s, gath_s, me_d, gs_send, gs_recv).start()
        forward(v, me_d)

        def fwd_step(k, carry):
            depth_copy(v, k, gath_f, gath_f, me_d, gf_send, gf_recv).wait()
            depth_copy(v, k, gath_s, gath_s, me_d, gs_send, gs_recv).wait()
            forward(v, lax.rem(me_d + layers - k, layers))
            return carry

        lax.fori_loop(1, layers, fwd_step, 0)
        combine(v)

        def bwd_step(k, carry):
            e = depth_peer(k)
            backward(v, e)
            depth_copy(v, k, part_f, in_f, e, pf_send, pf_recv).start()
            depth_copy(v, k, part_s, in_s, e, ps_send, ps_recv).start()
            return carry

        lax.fori_loop(1, layers, bwd_step, 0)
        backward(v, me_d)
        sum_f = part_f[v, me_d].astype(f32)
        sum_s = part_s[v, me_d]
        for k in range(1, layers):
            e = depth_peer(k)
            depth_copy(v, k, part_f, in_f, e, pf_send, pf_recv).wait()
            depth_copy(v, k, part_s, in_s, e, ps_send, ps_recv).wait()
            origin = lax.rem(me_d + layers - k, layers)
            sum_f = sum_f + in_f[v, origin].astype(f32)
            sum_s = sum_s + in_s[v, origin]
        pack(
            back, v,
            jnp.concatenate(
                [
                    dot(place_t[v], sum_f.astype(bf16)),
                    dot(place_t[v], aux_rows(sum_s), 1, 1),
                ],
                axis=1,
            ),
        )
        exchange(v, back, ret, b_send, b_recv)
        returned = unpack(ret, v).astype(bf16)
        grad_feat = dot(perm[v], returned[:, :feats], 0, 0)
        grad_rows = dot(returned[:, feats:], perm[v], 0, 0)
        grad_eight = grad_rows[0:8] + grad_rows[8:16] + grad_rows[16:24]
        sg_ref[v] = grad_eight
        cur_f[...] = (cur_f[...].astype(f32) - feature_rate * grad_feat).astype(bf16)
        cur_l[...] = cur_l[...] - opacity_rate * grad_eight[5:6]

    newf_ref[...] = cur_f[...]
    newl_ref[...] = cur_l[...]


def body(features, logits, geometry, dest_slot, target):
    owners = lax.axis_size("tile")
    layers = lax.axis_size("depth")
    depth_here = lax.axis_index("depth")
    views, tiles, feats, pixels = target.shape
    owned = features.shape[1]
    cap = owned // owners
    share = pixels // layers
    wire = bf16 if cap % 16 == 0 else f32
    own_target = lax.dynamic_slice_in_dim(target, depth_here * share, share, 3)
    own_target = own_target.transpose(0, 1, 3, 2)
    geom = jnp.pad(geometry[:, 0], ((0, 0), (0, 3), (0, 0)))
    vm = pl.BlockSpec(memory_space=pltpu.VMEM)
    grid = (layers, tiles, share, S)
    dma = pltpu.SemaphoreType.DMA
    images, new_f, new_l, grads = pl.pallas_call(
        functools.partial(splat_kernel, owners, layers, views, tiles, share),
        out_shape=(
            jax.ShapeDtypeStruct((views, tiles, share, feats), bf16),
            jax.ShapeDtypeStruct((owned, feats), bf16),
            jax.ShapeDtypeStruct((1, owned), f32),
            jax.ShapeDtypeStruct((views, 8, owned), f32),
        ),
        in_specs=[vm] * 5,
        out_specs=(vm,) * 4,
        scratch_shapes=[
            pltpu.VMEM((views, owners, cap, 2 * feats), wire),
            pltpu.VMEM((views, owners, cap, 2 * feats), wire),
            pltpu.VMEM((views, owners, cap, 2 * feats), wire),
            pltpu.VMEM((views, owners, cap, 2 * feats), wire),
            pltpu.VMEM((views, layers, owned, feats), bf16),
            pltpu.VMEM((views, layers, 8, owned), f32),
            pltpu.VMEM((views, layers, owned, feats), bf16),
            pltpu.VMEM((views, layers, 8, owned), f32),
            pltpu.VMEM((views, layers, owned, feats), bf16),
            pltpu.VMEM((views, layers, 8, owned), f32),
            pltpu.VMEM((views, owned, owned), bf16),
            pltpu.VMEM((views, owned, owned), bf16),
            pltpu.VMEM((2, share, S), f32),
            pltpu.VMEM((2 * S, 2 * S), bf16),
            pltpu.VMEM((2 * S, S), bf16),
            pltpu.VMEM((2 * feats, feats), bf16),
            pltpu.VMEM(grid, f32),
            pltpu.VMEM(grid, f32),
            pltpu.VMEM(grid, bf16),
            pltpu.VMEM(grid, f32),
            pltpu.VMEM(grid, f32),
            pltpu.VMEM(grid, f32),
            pltpu.VMEM(grid, f32),
            pltpu.VMEM((tiles, share, feats), f32),
            pltpu.VMEM((share, feats), f32),
            pltpu.VMEM((owned, feats), bf16),
            pltpu.VMEM((1, owned), f32),
            dma((views, owners)), dma((views, owners)),
            dma((views, layers)), dma((views, layers)),
            dma((views, layers)), dma((views, layers)),
            dma((views, layers)), dma((views, layers)),
            dma((views, layers)), dma((views, layers)),
            dma((views, owners)), dma((views, owners)),
        ],
        compiler_params=pltpu.CompilerParams(
            collective_id=0, has_side_effects=True, vmem_limit_bytes=56 * 1024 * 1024
        ),
        name="splat_views",
    )(features[0], logits, geom, dest_slot, own_target)
    return (
        images.transpose(0, 1, 3, 2),
        new_f[None],
        new_l,
        grads[:, None, :5, :],
    )


def solution(mesh):
    placed = (
        P("depth", "tile", None),
        P("depth", "tile"),
        P(None, "depth", None, "tile"),
        P(None, "depth", "tile"),
        P(None, "tile", None, None),
    )
    return jax.shard_map(
        body,
        mesh=mesh,
        in_specs=placed,
        out_specs=(
            P(None, "tile", None, "depth"),
            P("depth", "tile", None),
            P("depth", "tile"),
            P(None, "depth", None, "tile"),
        ),
        check_vma=False,
    )
```

time: 310 us -> 66.9 us (0.22)
  waiting for transfers between devices: 123 us -> 0 us
  Pallas kernels: 0 us -> 60.1 us
  blocking collectives: 53.2 us -> 0 us
  starting transfers between devices: 36.2 us -> 0 us
  local copies, waits for them, and re-layouts: 35.9 us -> 5.96 us
  matrix products: 22.2 us -> 0 us
  other arithmetic: 21.8 us -> 0 us
  between operations: 14.7 us -> 0.69 us
    psum x2 -> x0, waiting for transfers between devices: 97.4 us -> none  [body(): summed = lax.psum(contrib, 'depth')]
    pallas_call x0 -> x1, Pallas kernels: none -> 60.1 us  [body(): pl.pallas_call(functools.partial(splat_kernel, owners, layers, views, til...]
    all_gather x4 -> x0, blocking collectives: 53.2 us -> none  [the longest x2 26.7 us: body(): all_terms = lax.all_gather(pixel_terms[None], 'depth', axis=0, tiled=True)]
    all_to_all x10 -> x0, starting transfers between devices: 36.1 us -> none  [the longest x2 8.64 us: body(): lax.all_to_all(slot_buffer, 'tile', split_axis=0, concat_axis=0, tiled=True)]
    all_to_all x10 -> x0, waiting for transfers between devices: 26 us -> none  [the longest x2 6.97 us: body(): lax.all_to_all(back_shape, 'tile', split_axis=0, concat_axis=0, tiled=True)]
    dot_general x24 -> x0, matrix products: 22.2 us -> none  [the longest x12 15.4 us: block_sum(): jnp.einsum('ij,bjp->bip', triangle, blocks, precision=lax.Precision.HIGHEST)]
    scatter x9 -> x0, local copies, waits for them, and re-layouts: 11 us -> none  [the longest x2 2.79 us: body(): slot_buffer = jnp.full((owners * capacity + 1,), -1, jnp.int32).at[positi...]
    reduce_sum x16 -> x0, other arithmetic: 8.85 us -> none  [the longest x8 4.04 us: block_sum(): block_totals = jnp.sum(blocks, axis=1)]
  transfers between devices with their start and end apart: 12 -> 0, of which waited for: 12 -> 0; matrix products, arithmetic and copies ran while one was open for 8% -> 0% of each run, Pallas kernels for 0% -> 0%
where the time goes in v1:
time: 66.9 us; the launch traced here: 66.7 us
  Pallas kernels  60.1 us (90%)
  local copies, waits for them, and re-layouts  5.96 us (9%)
  between operations  0.69 us (1%)
    pallas_call x1, Pallas kernels, body(): pl.pallas_call(functools.partial(splat_kernel, owners, layers, views, til...  60.1 us
    unnamed x16, local copies, waits for them, and re-layouts  5.31 us

profile of v1, /device:TPU:0, one launch (start us, length us, event | category | flops | bytes accessed | tf_op | source)
XLA Modules:
  0.0 66.7 jit_solution(10171273056772125711)
XLA Ops:
  0.6 0.0 copy-start
  0.6 0.0 copy-start.3
  0.7 0.8 %copy-done.3 = f32[2,1,5,256]{3,1,2,0:T(1,128)S(1)} copy-done((f32[2,1,5,256]{3,1,2,0:T(1,128)S(1)}, f32[2,1,5,256]{3,1,2,0:T(1,128)}, u32[]{:S(2)}) %copy-start.3) | copy-done | bytes 10264
  1.4 0.6 pad.4.geom_ref
  2.1 0.0 copy-done
  2.1 0.8 %copy.17 = bf16[2,2,128,256]{2,3,1,0:T(8,128)(2,1)} copy(bf16[2,2,128,256]{3,2,1,0:T(8,128)(2,1)S(1)} %constant_dynamic-slice_fusion) | data formatting | bytes 524288
  2.9 60.1 %splat_views.1 = (bf16[2,2,256,128]{3,2,1,0:T(8,128)(2,1)}, bf16[256,128]{1,0:T(8,128)(2,1)}, f32[1,256]{1,0:T(1,128)}, f32[2,8,256]{2,1,0:T(8,128)}) custom-call(bf16[256,128]{1,0:T(8,128)(2,1)} %bitcast.12, f32[1,256]{1,0:T(1,128)} %logit_ref.1, f32[2,8,256]{2,1,0:T(8,128)} %pad.4.geom_ref, s32[2,1,256]{2,1,0:T(1,128)} %dest_ref.1, ...), custom_call_target="tpu_custom_call" | custom-call | tf_op jit(solution)/shard_map/splat_views/pallas_call | solution.py:328
  63.0 0.0 copy-start.2
  63.0 0.0 copy-start.1
  63.0 1.8 %copy.15 = bf16[2,2,128,256]{3,2,1,0:T(8,128)(2,1)} copy(bf16[2,2,128,256]{2,3,1,0:T(8,128)(2,1)} %bitcast.10) | data formatting | bytes 524288
  64.9 0.0 copy-done.2
  64.9 0.6 copy.16
  65.5 0.0 copy-done.1
  65.5 0.0 copy-start.4
  65.5 0.6 copy.22
  66.1 0.0 copy-done.4
  66.1 0.6 copy.23
  (4 shorter events, 0.0 us)
Async XLA Ops:
  0.6 1.4 %copy-start = (bf16[2,2,128,1024]{3,2,1,0:T(8,128)(2,1)S(1)}, bf16[2,2,128,1024]{3,2,1,0:T(8,128)(2,1)}, u32[]{:S(2)}) copy-start(bf16[2,2,128,1024]{3,2,1,0:T(8,128)(2,1)} %param.9) | copy-start | bytes 3145732
  0.6 0.8 %copy-start.3 = (f32[2,1,5,256]{3,1,2,0:T(1,128)S(1)}, f32[2,1,5,256]{3,1,2,0:T(1,128)}, u32[]{:S(2)}) copy-start(f32[2,1,5,256]{3,1,2,0:T(1,128)} %param.7) | copy-start | bytes 30724
  63.0 1.8 %copy-start.2 = (f32[2,8,256]{2,1,0:T(8,128)S(1)}, f32[2,8,256]{2,1,0:T(8,128)}, u32[]{:S(2)}) copy-start(f32[2,8,256]{2,1,0:T(8,128)} %get-tuple-element.11) | copy-start | bytes 49156
  63.0 2.5 %copy-start.1 = (bf16[256,128]{1,0:T(8,128)(2,1)S(1)}, bf16[256,128]{1,0:T(8,128)(2,1)}, u32[]{:S(2)}) copy-start(bf16[256,128]{1,0:T(8,128)(2,1)} %get-tuple-element.9) | copy-start | bytes 196612
  65.5 0.7 copy-start.4

commit v2 on v1

v2 whole, which is shorter than its diff:
```python
import functools

import jax
import jax.numpy as jnp
from jax import lax
from jax.experimental import pallas as pl
from jax.experimental.pallas import tpu as pltpu
from jax.sharding import PartitionSpec as P

W = 32
S = 128
clamp_top = 0.99
feature_rate = 0.5
opacity_rate = 0.5
f32 = jnp.float32
bf16 = jnp.bfloat16


def dot(lhs, rhs, left=1, right=0):
    return lax.dot_general(
        lhs, rhs, (((left,), (right,)), ((), ())), preferred_element_type=f32
    )


def three_parts(value):
    high = value.astype(bf16).astype(f32)
    rest = value - high
    mid = rest.astype(bf16).astype(f32)
    return high, mid, rest - mid


def two_parts(value):
    high = value.astype(bf16)
    low = (value - high.astype(f32)).astype(bf16)
    return jnp.concatenate([high, low], axis=1)


def iota(shape, axis):
    return lax.broadcasted_iota(jnp.int32, shape, axis)


def put_rows(rows, shape):
    place = iota(shape, 0)
    total = jnp.zeros(shape, f32)
    for at, row in enumerate(rows):
        total = jnp.where(place == at, row, total)
    return total


def splat_kernel(
    owners, layers, views, tiles, share,
    feat_ref, logit_ref, geom_ref, dest_ref, target_ref,
    img_ref, newf_ref, newl_ref, sg_ref,
    pay, got, back, ret, mine_f, mine_s, gath_f, gath_s, part_f, part_s, in_f, in_s,
    img_out, img_in, perm, ids, place_t, places, tri, tril, ones2,
    fall_s, dec_s, w_s, comp_s, keep_s, ahead_s, gk_s, res_s, run_s,
    cur_f, cur_l,
    a_send, a_recv, gf_send, gf_recv, gs_send, gs_recv,
    pf_send, pf_recv, ps_send, ps_recv, b_send, b_recv, i_send, i_recv,
):
    me_t = lax.axis_index("tile")
    me_d = lax.axis_index("depth")
    owned, feats = feat_ref.shape
    cap = owned // owners
    wire = pay.dtype
    group = layers // tiles
    pixels = tiles * share
    my_tile = me_d // group
    partner = lax.rem(me_d + group, layers)

    def tile_peer(k):
        return lax.rem(me_t + k, owners)

    def depth_peer(k):
        return lax.rem(me_d + k, layers)

    barrier = pltpu.get_barrier_semaphore()
    for k in range(1, owners):
        pl.semaphore_signal(barrier, inc=1, device_id=(tile_peer(k), me_d), device_id_type=pl.DeviceIdType.MESH)
    for k in range(1, layers):
        pl.semaphore_signal(barrier, inc=1, device_id=(me_t, depth_peer(k)), device_id_type=pl.DeviceIdType.MESH)

    lane_row = iota((pixels, S), 0)
    pixel = lane_row + jnp.where(lane_row < share, me_d, partner - 1) * share
    places[0] = (pixel & (W - 1)).astype(f32) + 0.5
    places[1] = (pixel >> (W.bit_length() - 1)).astype(f32) + 0.5
    row = iota((S, S), 0)
    col = iota((S, S), 1)
    earlier = (row < col).astype(f32).astype(bf16)
    later_mat = (row > col).astype(f32).astype(bf16)
    ones = jnp.ones((S, S), bf16)
    half = jnp.concatenate([earlier, ones], axis=1)
    tri[...] = jnp.concatenate([half, half], axis=0)
    tril[...] = jnp.concatenate([later_mat, later_mat], axis=0)
    ones2[...] = jnp.ones((2 * feats, feats), bf16)
    cur_f[...] = feat_ref[...]
    cur_l[...] = logit_ref[...]

    def tile_copy(v, k, src, dst, send, recv):
        return pltpu.make_async_remote_copy(
            src_ref=src.at[v, tile_peer(k)], dst_ref=dst.at[v, me_t],
            send_sem=send.at[v, k], recv_sem=recv.at[v, k],
            device_id=(tile_peer(k), me_d), device_id_type=pl.DeviceIdType.MESH,
        )

    def exchange(v, src, dst, send, recv, beside=None):
        for k in range(1, owners):
            tile_copy(v, k, src, dst, send, recv).start()
        dst[v, me_t] = src[v, me_t]
        if beside is not None:
            beside()
        for k in range(1, owners):
            tile_copy(v, k, src, dst, send, recv).wait()

    def depth_copy(v, k, src, dst, src_at, send, recv):
        return pltpu.make_async_remote_copy(
            src_ref=src.at[v, src_at], dst_ref=dst.at[v, me_d],
            send_sem=send.at[v, k], recv_sem=recv.at[v, k],
            device_id=(me_t, depth_peer(k)), device_id_type=pl.DeviceIdType.MESH,
        )

    def image_copy(v):
        return pltpu.make_async_remote_copy(
            src_ref=img_out.at[v], dst_ref=img_in.at[v],
            send_sem=i_send.at[v], recv_sem=i_recv.at[v],
            device_id=(me_t, partner), device_id_type=pl.DeviceIdType.MESH,
        )

    def slot_rows(v, e):
        g = gath_s[v, e]
        coef_a = jnp.exp(g[2:3])
        coef_c = jnp.exp(g[3:4])
        spread = jnp.exp(0.5 * (g[2:3] + g[3:4]))
        return g[0:1], g[1:2], coef_a, g[4:5] * spread, coef_c, spread, g[5:6]

    def forward(v, e):
        g0, g1, ca, cb, cc, _, opacity = slot_rows(v, e)
        dx = places[0] - g0
        dy = places[1] - g1
        quadric = ca * dx * dx + 2.0 * cb * dx * dy + cc * dy * dy
        fall = jnp.exp(-0.5 * quadric)
        coverage = jnp.minimum(opacity * fall, clamp_top)
        log_keep = jnp.log(1.0 - coverage)
        sums = dot(two_parts(log_keep), tri[...])
        decayed = jnp.exp(sums[:, :S])
        weights = (coverage * decayed).astype(bf16)
        fall_s[e] = fall
        dec_s[e] = decayed
        w_s[e] = weights
        keep_s[e] = jnp.exp(sums[:, S:])
        comp_s[e] = dot(weights, gath_f[v, e])

    def combine(v):
        res_s[...] = jnp.zeros((pixels, feats), f32)
        run_s[...] = jnp.ones((pixels, feats), f32)

        def front(e, carry):
            ahead = run_s[...]
            ahead_s[e] = ahead
            res_s[...] = res_s[...] + ahead * comp_s[e]
            run_s[...] = ahead * keep_s[e]
            return carry

        lax.fori_loop(0, layers, front, 0)
        summed = res_s[...]
        img_ref[v, my_tile] = summed[:share].T.astype(bf16)
        img_out[v] = summed[share:].T.astype(bf16)
        res_s[...] = summed - target_ref[v].astype(f32)
        run_s[...] = jnp.zeros((pixels, feats), f32)

        def rear(i, carry):
            e = layers - 1 - i
            behind = run_s[...]
            keep = keep_s[e]
            gk_s[e] = ahead_s[e] * behind * keep
            terms = dot(two_parts(res_s[...] * comp_s[e]), ones2[...])
            run_s[...] = terms + keep * behind
            return carry

        lax.fori_loop(0, layers, rear, 0)

    def backward(v, e, out_f, out_s):
        g0, g1, ca, cb, cc, spread, opacity = slot_rows(v, e)
        grad_comp = (ahead_s[e] * res_s[...]).astype(bf16)
        out_f[v, e] = dot(w_s[e], grad_comp, 0, 0).astype(bf16)
        grad_weight = dot(grad_comp, gath_f[v, e], 1, 1)
        decayed = dec_s[e]
        fall = fall_s[e]
        product = opacity * fall
        coverage = jnp.minimum(product, clamp_top)
        grad_decayed = grad_weight * decayed
        later = dot(two_parts(grad_decayed * coverage), tril[...])
        grad_log = later + gk_s[e]
        grad_coverage = grad_decayed - grad_log / (1.0 - coverage)
        moment = fall * jnp.where(product < clamp_top, grad_coverage, 0.0)
        dx = places[0] - g0
        dy = places[1] - g1
        moment_x = moment * dx
        moment_y = moment * dy

        def total(value):
            return jnp.sum(value, axis=0, keepdims=True)

        m0 = total(moment)
        mx = opacity * total(moment_x)
        my = opacity * total(moment_y)
        first = -0.5 * opacity * total(moment_x * dx)
        cross = -1.0 * opacity * total(moment_x * dy)
        second = -0.5 * opacity * total(moment_y * dy)
        out_s[v, e] = put_rows(
            [
                ca * mx + cb * my,
                cb * mx + cc * my,
                ca * first + 0.5 * cb * cross,
                cc * second + 0.5 * cb * cross,
                spread * cross,
                opacity * (1.0 - opacity) * m0,
            ],
            (8, S),
        )

    def aux_rows(eight):
        high, mid, low = three_parts(eight)
        zero = jnp.zeros((feats - 24, owned), f32)
        return jnp.concatenate([high, mid, low, zero], axis=0).astype(bf16)

    def pack(ref, v, value):
        ref[v] = value.reshape(owners, cap, value.shape[1]).astype(wire)

    def unpack(ref, v):
        return ref[v].astype(f32).reshape(owners * cap, 2 * feats)

    def indices(v):
        dest = dest_ref[v]
        low_edge = iota((owners, owned), 0) * owned
        hit = (dest >= low_edge) & (dest < low_edge + owned)
        matches = hit.astype(f32)
        upper = (iota((owned, owned), 0) < iota((owned, owned), 1)).astype(f32).astype(bf16)
        rank = dot(matches.astype(bf16), upper)
        count = iota((owners, owned), 0).astype(f32) * cap + rank + 1.0
        position = jnp.sum(matches * count, axis=0, keepdims=True) - 1.0
        ids[v] = jnp.sum(
            matches * (dest - low_edge + 1).astype(f32), axis=0, keepdims=True
        )
        perm[v] = (iota((owned, owned), 0).astype(f32) == position).astype(f32).astype(bf16)

    def dispatch(v):
        opacity = 1.0 / (1.0 + jnp.exp(-cur_l[...]))
        rows8 = iota((8, owned), 0)
        eight = jnp.where(rows8 == 5, opacity, jnp.where(rows8 == 6, ids[v], geom_ref[v]))
        pack(
            pay, v,
            jnp.concatenate(
                [dot(perm[v], cur_f[...]), dot(perm[v], aux_rows(eight), 1, 1)], axis=1
            ),
        )

    def later_indices():
        for v in range(1, views):
            indices(v)

    indices(0)
    for v in range(views):
        dispatch(v)
        if v == 0:
            pl.semaphore_wait(barrier, owners + layers - 2)
        exchange(v, pay, got, a_send, a_recv, later_indices if v == 0 else None)

        arrived = unpack(got, v)
        aux = arrived[:, feats:]
        aux_t = aux.T
        to_slot = (iota((owned, owned), 0).astype(f32) + 1.0 == aux_t[6:7, :]).astype(f32).astype(bf16)
        place_t[v] = (iota((owned, owned), 1).astype(f32) + 1.0 == aux[:, 6:7]).astype(f32).astype(bf16)
        slot_f = dot(to_slot, arrived[:, :feats].astype(bf16)).astype(bf16)
        shapes = dot(aux_t[0:32].astype(bf16), to_slot, 1, 1)
        shapes = shapes[0:8] + shapes[8:16] + shapes[16:24]
        for t in range(tiles):
            mine_f[v, t] = slot_f[t * S : (t + 1) * S]
            mine_s[v, t] = shapes[:, t * S : (t + 1) * S]

        def gather(k):
            there = depth_peer(k) // group
            return (
                depth_copy(v, k, mine_f, gath_f, there, gf_send, gf_recv),
                depth_copy(v, k, mine_s, gath_s, there, gs_send, gs_recv),
            )

        for k in range(1, layers):
            for copy in gather(k):
                copy.start()
        gath_f[v, me_d] = mine_f[v, my_tile]
        gath_s[v, me_d] = mine_s[v, my_tile]
        forward(v, me_d)

        def fwd_step(k, carry):
            for copy in gather(k):
                copy.wait()
            forward(v, lax.rem(me_d + layers - k, layers))
            return carry

        lax.fori_loop(1, layers, fwd_step, 0)
        combine(v)

        def give(k):
            e = depth_peer(k)
            return (
                depth_copy(v, k, part_f, in_f, e, pf_send, pf_recv),
                depth_copy(v, k, part_s, in_s, e, ps_send, ps_recv),
            )

        def bwd_step(k, carry):
            backward(v, depth_peer(k), part_f, part_s)
            for copy in give(k):
                copy.start()
            return carry

        lax.fori_loop(1, layers, bwd_step, 0)
        backward(v, me_d, in_f, in_s)
        for k in range(1, layers):
            for copy in give(k):
                copy.wait()
        image_copy(v).start()
        sums_f = []
        sums_s = []
        for t in range(tiles):
            sums_f.append(sum(in_f[v, z].astype(f32) for z in range(t * group, (t + 1) * group)))
            sums_s.append(sum(in_s[v, z] for z in range(t * group, (t + 1) * group)))
        sum_f = jnp.concatenate(sums_f, axis=0)
        sum_s = jnp.concatenate(sums_s, axis=1)
        pack(
            back, v,
            jnp.concatenate(
                [
                    dot(place_t[v], sum_f.astype(bf16)),
                    dot(place_t[v], aux_rows(sum_s), 1, 1),
                ],
                axis=1,
            ),
        )
        exchange(v, back, ret, b_send, b_recv)
        returned = unpack(ret, v).astype(bf16)
        grad_feat = dot(perm[v], returned[:, :feats], 0, 0)
        grad_rows = dot(returned[:, feats:], perm[v], 0, 0)
        grad_eight = grad_rows[0:8] + grad_rows[8:16] + grad_rows[16:24]
        sg_ref[v] = grad_eight
        cur_f[...] = (cur_f[...].astype(f32) - feature_rate * grad_feat).astype(bf16)
        cur_l[...] = cur_l[...] - opacity_rate * grad_eight[5:6]

    for v in range(views):
        image_copy(v).wait()
        img_ref[v, 1 - my_tile] = img_in[v]
    newf_ref[...] = cur_f[...]
    newl_ref[...] = cur_l[...]


def body(features, logits, geometry, dest_slot, target):
    owners = lax.axis_size("tile")
    layers = lax.axis_size("depth")
    depth_here = lax.axis_index("depth")
    views, tiles, feats, pixels = target.shape
    owned = features.shape[1]
    cap = owned // owners
    share = pixels // layers
    wire = bf16 if cap % 16 == 0 else f32
    if tiles != 2 or layers % tiles or owned > 256:
        raise ValueError("unsupported split")
    group = layers // tiles
    tile_here = depth_here // group
    partner = lax.rem(depth_here + group, layers)
    own_target = jnp.concatenate(
        [
            lax.dynamic_slice(target, (0, tile_here, 0, place * share), (views, 1, feats, share))[:, 0]
            for place in (depth_here, partner)
        ],
        axis=2,
    ).transpose(0, 2, 1)
    geom = jnp.pad(geometry[:, 0], ((0, 0), (0, 3), (0, 0)))
    vm = pl.BlockSpec(memory_space=pltpu.VMEM)
    grid = (layers, tiles * share, S)
    dma = pltpu.SemaphoreType.DMA
    images, new_f, new_l, grads = pl.pallas_call(
        functools.partial(splat_kernel, owners, layers, views, tiles, share),
        out_shape=(
            jax.ShapeDtypeStruct((views, tiles, feats, share), bf16),
            jax.ShapeDtypeStruct((owned, feats), bf16),
            jax.ShapeDtypeStruct((1, owned), f32),
            jax.ShapeDtypeStruct((views, 8, owned), f32),
        ),
        in_specs=[vm] * 5,
        out_specs=(vm,) * 4,
        scratch_shapes=[
            pltpu.VMEM((views, owners, cap, 2 * feats), wire),
            pltpu.VMEM((views, owners, cap, 2 * feats), wire),
            pltpu.VMEM((views, owners, cap, 2 * feats), wire),
            pltpu.VMEM((views, owners, cap, 2 * feats), wire),
            pltpu.VMEM((views, tiles, S, feats), bf16),
            pltpu.VMEM((views, tiles, 8, S), f32),
            pltpu.VMEM((views, layers, S, feats), bf16),
            pltpu.VMEM((views, layers, 8, S), f32),
            pltpu.VMEM((views, layers, S, feats), bf16),
            pltpu.VMEM((views, layers, 8, S), f32),
            pltpu.VMEM((views, layers, S, feats), bf16),
            pltpu.VMEM((views, layers, 8, S), f32),
            pltpu.VMEM((views, feats, share), bf16),
            pltpu.VMEM((views, feats, share), bf16),
            pltpu.VMEM((views, owned, owned), bf16),
            pltpu.VMEM((views, 1, owned), f32),
            pltpu.VMEM((views, owned, owned), bf16),
            pltpu.VMEM((2, tiles * share, S), f32),
            pltpu.VMEM((2 * S, 2 * S), bf16),
            pltpu.VMEM((2 * S, S), bf16),
            pltpu.VMEM((2 * feats, feats), bf16),
            pltpu.VMEM(grid, f32),
            pltpu.VMEM(grid, f32),
            pltpu.VMEM(grid, bf16),
            pltpu.VMEM(grid, f32),
            pltpu.VMEM(grid, f32),
            pltpu.VMEM(grid, f32),
            pltpu.VMEM(grid, f32),
            pltpu.VMEM((tiles * share, feats), f32),
            pltpu.VMEM((tiles * share, feats), f32),
            pltpu.VMEM((owned, feats), bf16),
            pltpu.VMEM((1, owned), f32),
            dma((views, owners)), dma((views, owners)),
            dma((views, layers)), dma((views, layers)),
            dma((views, layers)), dma((views, layers)),
            dma((views, layers)), dma((views, layers)),
            dma((views, layers)), dma((views, layers)),
            dma((views, owners)), dma((views, owners)),
            dma((views,)), dma((views,)),
        ],
        compiler_params=pltpu.CompilerParams(
            collective_id=0, has_side_effects=True, vmem_limit_bytes=56 * 1024 * 1024
        ),
        name="splat_views",
    )(features[0], logits, geom, dest_slot, own_target)
    return (
        images,
        new_f[None],
        new_l,
        grads[:, None, :5, :],
    )


def solution(mesh):
    placed = (
        P("depth", "tile", None),
        P("depth", "tile"),
        P(None, "depth", None, "tile"),
        P(None, "depth", "tile"),
        P(None, "tile", None, None),
    )
    return jax.shard_map(
        body,
        mesh=mesh,
        in_specs=placed,
        out_specs=(
            P(None, "tile", None, "depth"),
            P("depth", "tile", None),
            P("depth", "tile"),
            P(None, "depth", None, "tile"),
        ),
        check_vma=False,
    )
```

time: 66.9 us -> 57.2 us (0.86)
  Pallas kernels: 60.1 us -> 48.7 us
  local copies, waits for them, and re-layouts: 5.96 us -> 6.82 us
  other arithmetic: 0 us -> 0.72 us
    pallas_call x1, Pallas kernels: 60.1 us -> 48.7 us  [body(): pl.pallas_call(functools.partial(splat_kernel, owners, layers, views, til...]
    dynamic_slice x1 -> x3, local copies, waits for them, and re-layouts: 0.03 us -> 1.23 us  [body(): lax.dynamic_slice(target, (0, tile_here, 0, place * share), (views, 1, fe...]
    unnamed x16 -> x11, local copies, waits for them, and re-layouts: 5.31 us -> 4.25 us
    transpose x0 -> x1, other arithmetic: none -> 0.72 us  [body(): own_target = jnp.concatenate([lax.dynamic_slice(target, (0, tile_here, 0,...]
    broadcast_in_dim x1, local copies, waits for them, and re-layouts: 0.01 us -> 0.72 us  [body(): return (images, new_f[None], new_l, grads[:, None, :5, :])]
where the time goes in v2:
time: 57.2 us; the launch traced here: 56.9 us
  Pallas kernels  48.7 us (85%)
  local copies, waits for them, and re-layouts  6.82 us (12%)
  other arithmetic  0.72 us (1%)
  between operations  0.69 us (1%)
    pallas_call x1, Pallas kernels, body(): pl.pallas_call(functools.partial(splat_kernel, owners, layers, views, til...  48.7 us
    unnamed x11, local copies, waits for them, and re-layouts  4.25 us
    dynamic_slice x3, local copies, waits for them, and re-layouts, body(): lax.dynamic_slice(target, (0, tile_here, 0, place * share), (views, 1, fe...  1.23 us

profile of v2, /device:TPU:0, one launch (start us, length us, event | category | flops | bytes accessed | tf_op | source)
XLA Modules:
  0.0 56.9 jit_solution(4878648057813511341)
XLA Ops:
  0.6 0.0 copy-start.1
  0.7 0.7 %copy-done.1 = f32[2,1,5,256]{3,1,2,0:T(1,128)S(1)} copy-done((f32[2,1,5,256]{3,1,2,0:T(1,128)S(1)}, f32[2,1,5,256]{3,1,2,0:T(1,128)}, u32[]{:S(2)}) %copy-start.1) | copy-done | bytes 10264
  1.4 0.6 %pad.4.geom_ref = f32[2,8,256]{2,1,0:T(8,128)} pad(f32[2,5,256]{2,1,0:T(8,128)S(1)} %copy.13, f32[]{:T(128)} %constant.21.clone.1), padding=0_0x0_3x0_0 | pad | bytes 26628 | tf_op jit(solution)/shard_map/jit(_pad)/pad | solution.py:377
  2.0 1.0 %constant_dynamic-slice_fusion.1 = (bf16[2,1,128,256]{3,2,1,0:T(8,128)(2,1)S(1)}, bf16[2,1,128,256]{3,2,1,0:T(8,128)(2,1)S(1)}) fusion(bf16[2,2,128,1024]{3,2,1,0:T(8,128)(2,1)} %param.9, s32[]{:T(128)S(6)} %select_n.16, s32[]{:T(128)S(6)} %select_n.17, s32[]{:T(128)S(6)} %select_n.18), kind=kLoop, calls=%fused_computation.4 | loop fusion | bytes 524300 | tf_op jit(solution)/shard_map/dynamic_slice | solution.py:372
  3.0 0.1 copy.14
  3.1 0.1 copy.15
  3.2 0.7 %maximum_bitcast_fusion.target_ref = bf16[2,512,128]{2,1,0:T(8,128)(2,1)} fusion(bf16[2,128,256]{1,2,0:T(8,128)(2,1)S(1)} %bitcast.12, bf16[2,128,256]{1,2,0:T(8,128)(2,1)S(1)} %bitcast.11), kind=kLoop, calls=%fused_computation | loop fusion | flops 524288 | bytes 524288 | tf_op jit(solution)/shard_map/transpose | solution.py:376
  3.9 48.7 %splat_views.1 = (bf16[2,2,128,256]{3,2,1,0:T(8,128)(2,1)}, bf16[256,128]{1,0:T(8,128)(2,1)}, f32[1,256]{1,0:T(1,128)}, f32[2,8,256]{2,1,0:T(8,128)}) custom-call(bf16[256,128]{1,0:T(8,128)(2,1)} %bitcast.14, f32[1,256]{1,0:T(1,128)} %logit_ref.1, f32[2,8,256]{2,1,0:T(8,128)} %pad.4.geom_ref, s32[2,1,256]{2,1,0:T(1,128)} %dest_ref.1, ...), custom_call_target="tpu_custom_call" | custom-call | tf_op jit(solution)/shard_map/splat_views/pallas_call | solution.py:381
  52.6 0.7 %slice_bitcast_fusion = f32[2,1,5,256]{3,2,0,1:T(8,128)S(1)} fusion(f32[2,8,256]{2,1,0:T(8,128)} %get-tuple-element.11), kind=kLoop, calls=%fused_computation.1 | loop fusion | bytes 20480 | tf_op jit(solution)/shard_map/broadcast_in_dim | solution.py:441
  53.3 0.6 %copy.16 = f32[2,1,5,256]{3,1,2,0:T(1,128)} copy(f32[2,1,5,256]{3,2,0,1:T(8,128)S(1)} %slice_bitcast_fusion) | data formatting | bytes 20480
  54.0 0.0 copy-start
  54.0 1.7 %copy.22 = bf16[2,2,128,256]{3,2,1,0:T(8,128)(2,1)} copy(bf16[2,2,128,256]{3,2,1,0:T(8,128)(2,1)} %get-tuple-element.26) | data formatting | bytes 524288
  55.7 0.0 copy-done
  55.7 0.0 copy-start.2
  55.7 0.6 %copy.23 = bf16[1,256,128]{2,1,0:T(8,128)(2,1)} copy(bf16[1,256,128]{2,1,0:T(8,128)(2,1)S(1)} %bitcast.13) | data formatting | bytes 131072
  56.3 0.1 copy-done.2
  56.3 0.6 copy.24
  (2 shorter events, 0.0 us)
Async XLA Ops:
  0.6 0.7 %copy-start.1 = (f32[2,1,5,256]{3,1,2,0:T(1,128)S(1)}, f32[2,1,5,256]{3,1,2,0:T(1,128)}, u32[]{:S(2)}) copy-start(f32[2,1,5,256]{3,1,2,0:T(1,128)} %param.7) | copy-start | bytes 30724
  54.0 1.7 %copy-start = (bf16[256,128]{1,0:T(8,128)(2,1)S(1)}, bf16[256,128]{1,0:T(8,128)(2,1)}, u32[]{:S(2)}) copy-start(bf16[256,128]{1,0:T(8,128)(2,1)} %get-tuple-element.9) | copy-start | bytes 196612
  55.7 0.7 %copy-start.2 = (f32[1,256]{1,0:T(1,128)S(1)}, f32[1,256]{1,0:T(1,128)}, u32[]{:S(2)}) copy-start(f32[1,256]{1,0:T(1,128)} %get-tuple-element.28) | copy-start | bytes 3076

commit v3 on v2

--- a/solution.py
+++ b/solution.py
@@ -47,16 +47,25 @@
     return total
 
 
+def finish_kernel(img_ref, newf_ref, newl_ref, sg_ref, img_out, newf_out, newl_out, sg_out):
+    img_out[...] = img_ref[...]
+    newf_out[0] = newf_ref[...]
+    newl_out[...] = newl_ref[...]
+    for v in range(sg_ref.shape[0]):
+        sg_out[v, 0] = sg_ref[v, 0:5]
+
+
 def splat_kernel(
     owners, layers, views, tiles, share,
     feat_ref, logit_ref, geom_ref, dest_ref, target_ref,
     img_ref, newf_ref, newl_ref, sg_ref,
-    pay, got, back, ret, mine_f, mine_s, gath_f, gath_s, part_f, part_s, in_f, in_s,
-    img_out, img_in, perm, ids, place_t, places, tri, tril, ones2,
+    pay, got, back, ret, pay_s, got_s, back_s, ret_s, geom8, tgt, mine_f, mine_s, gath_f, gath_s, part_f, part_s, in_f, in_s,
+    img_out, img_in, perm, ids, to_slot, places, tri, tril, ones2,
     fall_s, dec_s, w_s, comp_s, keep_s, ahead_s, gk_s, res_s, run_s,
     cur_f, cur_l,
     a_send, a_recv, gf_send, gf_recv, gs_send, gs_recv,
     pf_send, pf_recv, ps_send, ps_recv, b_send, b_recv, i_send, i_recv,
+    as_send, as_recv, bs_send, bs_recv, load_sem,
 ):
     me_t = lax.axis_index("tile")
     me_d = lax.axis_index("depth")
@@ -65,6 +74,8 @@
     wire = pay.dtype
     group = layers // tiles
     pixels = tiles * share
+    lanes = 128
+    per = lanes // cap
     my_tile = me_d // group
     partner = lax.rem(me_d + group, layers)
 
@@ -79,6 +90,23 @@
         pl.semaphore_signal(barrier, inc=1, device_id=(tile_peer(k), me_d), device_id_type=pl.DeviceIdType.MESH)
     for k in range(1, layers):
         pl.semaphore_signal(barrier, inc=1, device_id=(me_t, depth_peer(k)), device_id_type=pl.DeviceIdType.MESH)
+
+    def target_copy(v, h):
+        if share % lanes == 0:
+            place = partner if h else me_d
+            source = target_ref.at[v, my_tile, :, pl.ds(pl.multiple_of(place * share, lanes), share)]
+        else:
+            source = target_ref.at[v, h]
+        return pltpu.make_async_copy(source, tgt.at[v, h], load_sem.at[1 + v * tiles + h])
+
+    feature_copy = pltpu.make_async_copy(feat_ref, cur_f, load_sem.at[0])
+    feature_copy.start()
+    for v in range(views):
+        for h in range(tiles):
+            target_copy(v, h).start()
+    for v in range(views):
+        geom8[v] = jnp.zeros((8, owned), f32)
+        geom8[v, 0:5] = geom_ref[v, 0]
 
     lane_row = iota((pixels, S), 0)
     pixel = lane_row + jnp.where(lane_row < share, me_d, partner - 1) * share
@@ -93,7 +121,6 @@
     tri[...] = jnp.concatenate([half, half], axis=0)
     tril[...] = jnp.concatenate([later_mat, later_mat], axis=0)
     ones2[...] = jnp.ones((2 * feats, feats), bf16)
-    cur_f[...] = feat_ref[...]
     cur_l[...] = logit_ref[...]
 
     def tile_copy(v, k, src, dst, send, recv):
@@ -103,14 +130,34 @@
             device_id=(tile_peer(k), me_d), device_id_type=pl.DeviceIdType.MESH,
         )
 
-    def exchange(v, src, dst, send, recv, beside=None):
+    def exchange(v, moves, beside=None):
         for k in range(1, owners):
-            tile_copy(v, k, src, dst, send, recv).start()
-        dst[v, me_t] = src[v, me_t]
+            for move in moves:
+                tile_copy(v, k, *move).start()
+        for src, dst, _, _ in moves:
+            dst[v, me_t] = src[v, me_t]
         if beside is not None:
             beside()
         for k in range(1, owners):
-            tile_copy(v, k, src, dst, send, recv).wait()
+            for move in moves:
+                tile_copy(v, k, *move).wait()
+
+    def spread(ref, v, eight):
+        for t in range(owners):
+            block = eight[:, (t // per) * lanes : (t // per + 1) * lanes]
+            turn = (t % per) * cap
+            ref[v, t] = pltpu.roll(block, lanes - turn, 1) if turn else block
+
+    def join(ref, v):
+        place = iota((8, lanes), 1) // cap
+        blocks = []
+        for first in range(0, owners, per):
+            block = ref[v, first]
+            for turn in range(1, per):
+                moved = pltpu.roll(ref[v, first + turn], turn * cap, 1)
+                block = jnp.where(place == turn, moved, block)
+            blocks.append(block)
+        return jnp.concatenate(blocks, axis=1)
 
     def depth_copy(v, k, src, dst, src_at, send, recv):
         return pltpu.make_async_remote_copy(
@@ -165,7 +212,11 @@
         summed = res_s[...]
         img_ref[v, my_tile] = summed[:share].T.astype(bf16)
         img_out[v] = summed[share:].T.astype(bf16)
-        res_s[...] = summed - target_ref[v].astype(f32)
+        for h in range(tiles):
+            target_copy(v, h).wait()
+            res_s[h * share : (h + 1) * share] = summed[
+                h * share : (h + 1) * share
+            ] - tgt[v, h].astype(f32).T
         run_s[...] = jnp.zeros((pixels, feats), f32)
 
         def rear(i, carry):
@@ -219,16 +270,17 @@
             (8, S),
         )
 
-    def aux_rows(eight):
+    def move_rows(eight, onehot, side):
         high, mid, low = three_parts(eight)
-        zero = jnp.zeros((feats - 24, owned), f32)
-        return jnp.concatenate([high, mid, low, zero], axis=0).astype(bf16)
+        rows = jnp.concatenate([high, mid, low, jnp.zeros_like(low)], axis=0)
+        moved = dot(rows.astype(bf16), onehot, 1, side)
+        return moved[0:8] + moved[8:16] + moved[16:24]
 
     def pack(ref, v, value):
-        ref[v] = value.reshape(owners, cap, value.shape[1]).astype(wire)
+        ref[v] = value.reshape(owners, cap, feats).astype(wire)
 
     def unpack(ref, v):
-        return ref[v].astype(f32).reshape(owners * cap, 2 * feats)
+        return ref[v].astype(f32).reshape(owned, feats).astype(bf16)
 
     def indices(v):
         dest = dest_ref[v]
@@ -247,33 +299,30 @@
     def dispatch(v):
         opacity = 1.0 / (1.0 + jnp.exp(-cur_l[...]))
         rows8 = iota((8, owned), 0)
-        eight = jnp.where(rows8 == 5, opacity, jnp.where(rows8 == 6, ids[v], geom_ref[v]))
-        pack(
-            pay, v,
-            jnp.concatenate(
-                [dot(perm[v], cur_f[...]), dot(perm[v], aux_rows(eight), 1, 1)], axis=1
-            ),
-        )
+        eight = jnp.where(rows8 == 5, opacity, jnp.where(rows8 == 6, ids[v], geom8[v]))
+        pack(pay, v, dot(perm[v], cur_f[...]))
+        spread(pay_s, v, move_rows(eight, perm[v], 1))
 
     def later_indices():
         for v in range(1, views):
             indices(v)
 
     indices(0)
+    feature_copy.wait()
     for v in range(views):
         dispatch(v)
         if v == 0:
             pl.semaphore_wait(barrier, owners + layers - 2)
-        exchange(v, pay, got, a_send, a_recv, later_indices if v == 0 else None)
-
-        arrived = unpack(got, v)
-        aux = arrived[:, feats:]
-        aux_t = aux.T
-        to_slot = (iota((owned, owned), 0).astype(f32) + 1.0 == aux_t[6:7, :]).astype(f32).astype(bf16)
-        place_t[v] = (iota((owned, owned), 1).astype(f32) + 1.0 == aux[:, 6:7]).astype(f32).astype(bf16)
-        slot_f = dot(to_slot, arrived[:, :feats].astype(bf16)).astype(bf16)
-        shapes = dot(aux_t[0:32].astype(bf16), to_slot, 1, 1)
-        shapes = shapes[0:8] + shapes[8:16] + shapes[16:24]
+        exchange(
+            v,
+            [(pay_s, got_s, as_send, as_recv), (pay, got, a_send, a_recv)],
+            later_indices if v == 0 else None,
+        )
+        arrived = join(got_s, v)
+        slots = (iota((owned, owned), 0).astype(f32) + 1.0 == arrived[6:7, :]).astype(f32).astype(bf16)
+        to_slot[v] = slots
+        slot_f = dot(slots, unpack(got, v)).astype(bf16)
+        shapes = move_rows(arrived, slots, 1)
         for t in range(tiles):
             mine_f[v, t] = slot_f[t * S : (t + 1) * S]
             mine_s[v, t] = shapes[:, t * S : (t + 1) * S]
@@ -327,21 +376,11 @@
             sums_s.append(sum(in_s[v, z] for z in range(t * group, (t + 1) * group)))
         sum_f = jnp.concatenate(sums_f, axis=0)
         sum_s = jnp.concatenate(sums_s, axis=1)
-        pack(
-            back, v,
-            jnp.concatenate(
-                [
-                    dot(place_t[v], sum_f.astype(bf16)),
-                    dot(place_t[v], aux_rows(sum_s), 1, 1),
-                ],
-                axis=1,
-            ),
-        )
-        exchange(v, back, ret, b_send, b_recv)
-        returned = unpack(ret, v).astype(bf16)
-        grad_feat = dot(perm[v], returned[:, :feats], 0, 0)
-        grad_rows = dot(returned[:, feats:], perm[v], 0, 0)
-        grad_eight = grad_rows[0:8] + grad_rows[8:16] + grad_rows[16:24]
+        pack(back, v, dot(to_slot[v], sum_f.astype(bf16), 0, 0))
+        spread(back_s, v, move_rows(sum_s, to_slot[v], 0))
+        exchange(v, [(back, ret, b_send, b_recv), (back_s, ret_s, bs_send, bs_recv)])
+        grad_feat = dot(perm[v], unpack(ret, v), 0, 0)
+        grad_eight = move_rows(join(ret_s, v), perm[v], 0)
         sg_ref[v] = grad_eight
         cur_f[...] = (cur_f[...].astype(f32) - feature_rate * grad_feat).astype(bf16)
         cur_l[...] = cur_l[...] - opacity_rate * grad_eight[5:6]
@@ -362,19 +401,22 @@
     cap = owned // owners
     share = pixels // layers
     wire = bf16 if cap % 16 == 0 else f32
-    if tiles != 2 or layers % tiles or owned > 256:
+    if tiles != 2 or layers % tiles or 128 % cap:
         raise ValueError("unsupported split")
-    group = layers // tiles
-    tile_here = depth_here // group
-    partner = lax.rem(depth_here + group, layers)
-    own_target = jnp.concatenate(
-        [
-            lax.dynamic_slice(target, (0, tile_here, 0, place * share), (views, 1, feats, share))[:, 0]
-            for place in (depth_here, partner)
-        ],
-        axis=2,
-    ).transpose(0, 2, 1)
-    geom = jnp.pad(geometry[:, 0], ((0, 0), (0, 3), (0, 0)))
+    if share % 128:
+        group = layers // tiles
+        tile_here = depth_here // group
+        partner = lax.rem(depth_here + group, layers)
+        target = jnp.concatenate(
+            [
+                lax.dynamic_slice(
+                    target, (0, tile_here, 0, place * share), (views, 1, feats, share)
+                )
+                for place in (depth_here, partner)
+            ],
+            axis=1,
+        )
+    hbm = pl.BlockSpec(memory_space=pl.ANY)
     vm = pl.BlockSpec(memory_space=pltpu.VMEM)
     grid = (layers, tiles * share, S)
     dma = pltpu.SemaphoreType.DMA
@@ -386,13 +428,19 @@
             jax.ShapeDtypeStruct((1, owned), f32),
             jax.ShapeDtypeStruct((views, 8, owned), f32),
         ),
-        in_specs=[vm] * 5,
+        in_specs=[hbm, vm, vm, vm, hbm],
         out_specs=(vm,) * 4,
         scratch_shapes=[
-            pltpu.VMEM((views, owners, cap, 2 * feats), wire),
-            pltpu.VMEM((views, owners, cap, 2 * feats), wire),
-            pltpu.VMEM((views, owners, cap, 2 * feats), wire),
-            pltpu.VMEM((views, owners, cap, 2 * feats), wire),
+            pltpu.VMEM((views, owners, cap, feats), wire),
+            pltpu.VMEM((views, owners, cap, feats), wire),
+            pltpu.VMEM((views, owners, cap, feats), wire),
+            pltpu.VMEM((views, owners, cap, feats), wire),
+            pltpu.VMEM((views, owners, 8, 128), f32),
+            pltpu.VMEM((views, owners, 8, 128), f32),
+            pltpu.VMEM((views, owners, 8, 128), f32),
+            pltpu.VMEM((views, owners, 8, 128), f32),
+            pltpu.VMEM((views, 8, owned), f32),
+            pltpu.VMEM((views, tiles, feats, share), bf16),
             pltpu.VMEM((views, tiles, S, feats), bf16),
             pltpu.VMEM((views, tiles, 8, S), f32),
             pltpu.VMEM((views, layers, S, feats), bf16),
@@ -428,18 +476,27 @@
             dma((views, layers)), dma((views, layers)),
             dma((views, owners)), dma((views, owners)),
             dma((views,)), dma((views,)),
+            dma((views, owners)), dma((views, owners)),
+            dma((views, owners)), dma((views, owners)),
+            dma((1 + views * tiles,)),
         ],
         compiler_params=pltpu.CompilerParams(
             collective_id=0, has_side_effects=True, vmem_limit_bytes=56 * 1024 * 1024
         ),
         name="splat_views",
-    )(features[0], logits, geom, dest_slot, own_target)
-    return (
-        images,
-        new_f[None],
-        new_l,
-        grads[:, None, :5, :],
-    )
+    )(features[0], logits, geometry, dest_slot, target)
+    return pl.pallas_call(
+        finish_kernel,
+        out_shape=(
+            jax.ShapeDtypeStruct(images.shape, bf16),
+            jax.ShapeDtypeStruct((1, owned, feats), bf16),
+            jax.ShapeDtypeStruct((1, owned), f32),
+            jax.ShapeDtypeStruct((views, 1, 5, owned), f32),
+        ),
+        in_specs=[vm] * 4,
+        out_specs=(vm,) * 4,
+        name="write_outputs",
+    )(images, new_f, new_l, grads)
 
 
 def solution(mesh):

time: 57.2 us -> 54.4 us (0.951)
  local copies, waits for them, and re-layouts: 6.82 us -> 2.64 us
  Pallas kernels: 48.7 us -> 50.6 us
  other arithmetic: 0.72 us -> 0 us
    unnamed x11 -> x1, local copies, waits for them, and re-layouts: 4.25 us -> 1.31 us
    pallas_call x0 -> x1, Pallas kernels: none -> 1.73 us  [body(): pl.pallas_call(finish_kernel, out_shape=(jax.ShapeDtypeStruct(images.shap...]
    pallas_call x0 -> x1, local copies, waits for them, and re-layouts: none -> 1.33 us  [body(): pl.pallas_call(finish_kernel, out_shape=(jax.ShapeDtypeStruct(images.shap...]
    dynamic_slice x3 -> x0, local copies, waits for them, and re-layouts: 1.23 us -> none  [body(): lax.dynamic_slice(target, (0, tile_here, 0, place * share), (views, 1, fe...]
    transpose x1 -> x0, other arithmetic: 0.72 us -> none  [body(): own_target = jnp.concatenate([lax.dynamic_slice(target, (0, tile_here, 0,...]
    broadcast_in_dim x1 -> x0, local copies, waits for them, and re-layouts: 0.72 us -> none  [body(): return (images, new_f[None], new_l, grads[:, None, :5, :])]
    pad x1 -> x0, local copies, waits for them, and re-layouts: 0.61 us -> none  [body(): geom = jnp.pad(geometry[:, 0], ((0, 0), (0, 3), (0, 0)))]
where the time goes in v3:
time: 54.4 us; the launch traced here: 53.9 us
  Pallas kernels  50.6 us (93%)
  local copies, waits for them, and re-layouts  2.64 us (5%)
  between operations  0.64 us (1%)
    pallas_call x1, Pallas kernels, body(): pl.pallas_call(functools.partial(splat_kernel, owners, layers, views, til...  48.9 us
    pallas_call x1, Pallas kernels, body(): pl.pallas_call(finish_kernel, out_shape=(jax.ShapeDtypeStruct(images.shap...  1.73 us
    pallas_call x1, local copies, waits for them, and re-layouts, body(): pl.pallas_call(finish_kernel, out_shape=(jax.ShapeDtypeStruct(images.shap...  1.33 us
    unnamed x1, local copies, waits for them, and re-layouts  1.31 us

profile of v3, /device:TPU:0, one launch (start us, length us, event | category | flops | bytes accessed | tf_op | source)
XLA Modules:
  0.0 53.9 jit_solution(18027535722564783540)
XLA Ops:
  0.6 1.3 %copy.9.geom_ref = f32[2,1,5,256]{3,2,1,0:T(8,128)} copy(f32[2,1,5,256]{3,1,2,0:T(1,128)} %param.7) | data formatting | bytes 20480 | tf_op args[2]
  1.9 48.9 %splat_views.1 = (bf16[2,2,128,256]{3,2,1,0:T(8,128)(2,1)}, bf16[256,128]{1,0:T(8,128)(2,1)}, f32[1,256]{1,0:T(1,128)}, f32[2,8,256]{2,1,0:T(8,128)}) custom-call(bf16[256,128]{1,0:T(8,128)(2,1)} %bitcast.1, f32[1,256]{1,0:T(1,128)} %logit_ref.1, f32[2,1,5,256]{3,2,1,0:T(8,128)} %copy.9.geom_ref, s32[2,1,256]{2,1,0:T(1,128)} %dest_ref.1, ...), custom_call_target="tpu_custom_call" | custom-call | tf_op jit(solution)/shard_map/splat_views/pallas_call | solution.py:423
  50.9 1.7 %write_outputs.1 = (bf16[2,2,128,256]{3,2,1,0:T(8,128)(2,1)}, bf16[1,256,128]{2,1,0:T(8,128)(2,1)}, f32[1,256]{1,0:T(1,128)}, f32[2,1,5,256]{3,2,1,0:T(8,128)}) custom-call(bf16[2,2,128,256]{3,2,1,0:T(8,128)(2,1)} %get-tuple-element.8.img_ref, bf16[256,128]{1,0:T(8,128)(2,1)} %get-tuple-element.9.newf_ref, f32[1,256]{1,0:T(1,128)} %get-tuple-element.10.newl_ref, ...), custom_call_target="tpu_custom_call" | custom-call | tf_op jit(solution)/shard_map/write_outputs/pallas_call | solution.py:488
  52.6 1.3 %copy.10 = f32[2,1,5,256]{3,1,2,0:T(1,128)} copy(f32[2,1,5,256]{3,2,1,0:T(8,128)} %get-tuple-element.15) | data formatting | bytes 20480 | tf_op jit(solution)/shard_map/write_outputs/pallas_call | solution.py:488

commit v4 on v3

--- a/solution.py
+++ b/solution.py
@@ -52,7 +52,24 @@
     newf_out[0] = newf_ref[...]
     newl_out[...] = newl_ref[...]
     for v in range(sg_ref.shape[0]):
-        sg_out[v, 0] = sg_ref[v, 0:5]
+        for r in range(5):
+            sg_out[v, r] = sg_ref[v, r : r + 1]
+
+
+def paired(me, k, count):
+    place, total = 1, 0
+    while place < count:
+        total = total + place * lax.rem(lax.div(me, place) + lax.rem(lax.div(k, place), 2), 2)
+        place *= 2
+    return total
+
+
+def steps(first, last, body):
+    if last - first <= 4:
+        for at in range(first, last):
+            body(at)
+    else:
+        lax.fori_loop(first, last, lambda at, carry: (body(at), carry)[1], 0)
 
 
 def splat_kernel(
@@ -80,10 +97,10 @@
     partner = lax.rem(me_d + group, layers)
 
     def tile_peer(k):
-        return lax.rem(me_t + k, owners)
+        return paired(me_t, k, owners)
 
     def depth_peer(k):
-        return lax.rem(me_d + k, layers)
+        return paired(me_d, k, layers)
 
     barrier = pltpu.get_barrier_semaphore()
     for k in range(1, owners):
@@ -106,7 +123,8 @@
             target_copy(v, h).start()
     for v in range(views):
         geom8[v] = jnp.zeros((8, owned), f32)
-        geom8[v, 0:5] = geom_ref[v, 0]
+        for r in range(5):
+            geom8[v, r : r + 1] = geom_ref[v, r]
 
     lane_row = iota((pixels, S), 0)
     pixel = lane_row + jnp.where(lane_row < share, me_d, partner - 1) * share
@@ -131,7 +149,7 @@
         )
 
     def exchange(v, moves, beside=None):
-        for k in range(1, owners):
+        for k in range(owners - 1, 0, -1):
             for move in moves:
                 tile_copy(v, k, *move).start()
         for src, dst, _, _ in moves:
@@ -201,14 +219,13 @@
         res_s[...] = jnp.zeros((pixels, feats), f32)
         run_s[...] = jnp.ones((pixels, feats), f32)
 
-        def front(e, carry):
+        def front(e):
             ahead = run_s[...]
             ahead_s[e] = ahead
             res_s[...] = res_s[...] + ahead * comp_s[e]
             run_s[...] = ahead * keep_s[e]
-            return carry
-
-        lax.fori_loop(0, layers, front, 0)
+
+        steps(0, layers, front)
         summed = res_s[...]
         img_ref[v, my_tile] = summed[:share].T.astype(bf16)
         img_out[v] = summed[share:].T.astype(bf16)
@@ -219,16 +236,16 @@
             ] - tgt[v, h].astype(f32).T
         run_s[...] = jnp.zeros((pixels, feats), f32)
 
-        def rear(i, carry):
+        def rear(i):
             e = layers - 1 - i
             behind = run_s[...]
             keep = keep_s[e]
             gk_s[e] = ahead_s[e] * behind * keep
             terms = dot(two_parts(res_s[...] * comp_s[e]), ones2[...])
             run_s[...] = terms + keep * behind
-            return carry
-
-        lax.fori_loop(0, layers, rear, 0)
+
+        steps(0, layers - 1, rear)
+        gk_s[0] = ahead_s[0] * run_s[...] * keep_s[0]
 
     def backward(v, e, out_f, out_s):
         g0, g1, ca, cb, cc, spread, opacity = slot_rows(v, e)
@@ -334,20 +351,20 @@
                 depth_copy(v, k, mine_s, gath_s, there, gs_send, gs_recv),
             )
 
-        for k in range(1, layers):
+        for k in range(layers - 1, 0, -1):
             for copy in gather(k):
                 copy.start()
         gath_f[v, me_d] = mine_f[v, my_tile]
         gath_s[v, me_d] = mine_s[v, my_tile]
         forward(v, me_d)
 
-        def fwd_step(k, carry):
+        def fwd_step(i):
+            k = layers - i
             for copy in gather(k):
                 copy.wait()
-            forward(v, lax.rem(me_d + layers - k, layers))
-            return carry
-
-        lax.fori_loop(1, layers, fwd_step, 0)
+            forward(v, depth_peer(k))
+
+        steps(1, layers, fwd_step)
         combine(v)
 
         def give(k):
@@ -357,13 +374,13 @@
                 depth_copy(v, k, part_s, in_s, e, ps_send, ps_recv),
             )
 
-        def bwd_step(k, carry):
+        def bwd_step(i):
+            k = layers - i
             backward(v, depth_peer(k), part_f, part_s)
             for copy in give(k):
                 copy.start()
-            return carry
-
-        lax.fori_loop(1, layers, bwd_step, 0)
+
+        steps(1, layers, bwd_step)
         backward(v, me_d, in_f, in_s)
         for k in range(1, layers):
             for copy in give(k):
@@ -401,7 +418,7 @@
     cap = owned // owners
     share = pixels // layers
     wire = bf16 if cap % 16 == 0 else f32
-    if tiles != 2 or layers % tiles or 128 % cap:
+    if tiles != 2 or layers % tiles or 128 % cap or layers & (layers - 1) or owners & (owners - 1):
         raise ValueError("unsupported split")
     if share % 128:
         group = layers // tiles
@@ -484,19 +501,20 @@
             collective_id=0, has_side_effects=True, vmem_limit_bytes=56 * 1024 * 1024
         ),
         name="splat_views",
-    )(features[0], logits, geometry, dest_slot, target)
-    return pl.pallas_call(
+    )(features[0], logits, geometry.transpose(0, 2, 1, 3), dest_slot, target)
+    images, new_f, new_l, grads = pl.pallas_call(
         finish_kernel,
         out_shape=(
             jax.ShapeDtypeStruct(images.shape, bf16),
             jax.ShapeDtypeStruct((1, owned, feats), bf16),
             jax.ShapeDtypeStruct((1, owned), f32),
-            jax.ShapeDtypeStruct((views, 1, 5, owned), f32),
+            jax.ShapeDtypeStruct((views, 5, 1, owned), f32),
         ),
         in_specs=[vm] * 4,
         out_specs=(vm,) * 4,
         name="write_outputs",
     )(images, new_f, new_l, grads)
+    return images, new_f, new_l, grads.transpose(0, 2, 1, 3)
 
 
 def solution(mesh):

time: 54.4 us -> 49.8 us (0.915)
  local copies, waits for them, and re-layouts: 2.64 us -> 0 us
  Pallas kernels: 50.6 us -> 49 us
    pallas_call x1, Pallas kernels: 48.9 us -> 47.2 us  [body(): pl.pallas_call(functools.partial(splat_kernel, owners, layers, views, til...]
    pallas_call x1 -> x0, local copies, waits for them, and re-layouts: 1.33 us -> none  [body(): pl.pallas_call(finish_kernel, out_shape=(jax.ShapeDtypeStruct(images.shap...]
    unnamed x1 -> x0, local copies, waits for them, and re-layouts: 1.31 us -> none
where the time goes in v4:
time: 49.8 us; the launch traced here: 49.6 us
  Pallas kernels  49 us (98%)
  between operations  0.64 us (1%)
    pallas_call x1, Pallas kernels, body(): pl.pallas_call(functools.partial(splat_kernel, owners, layers, views, til...  47.2 us
    pallas_call x1, Pallas kernels, body(): pl.pallas_call(finish_kernel, out_shape=(jax.ShapeDtypeStruct(images.shap...  1.73 us

profile of v4, /device:TPU:0, one launch (start us, length us, event | category | flops | bytes accessed | tf_op | source)
XLA Modules:
  0.0 49.6 jit_solution(3303484719021610927)
XLA Ops:
  0.6 47.2 %splat_views.1 = (bf16[2,2,128,256]{3,2,1,0:T(8,128)(2,1)}, bf16[256,128]{1,0:T(8,128)(2,1)}, f32[1,256]{1,0:T(1,128)}, f32[2,8,256]{2,1,0:T(8,128)}) custom-call(bf16[256,128]{1,0:T(8,128)(2,1)} %bitcast.3, f32[1,256]{1,0:T(1,128)} %logit_ref.1, f32[2,5,1,256]{3,2,1,0:T(1,128)} %bitcast.4, s32[2,1,256]{2,1,0:T(1,128)} %dest_ref.1, ...), custom_call_target="tpu_custom_call" | custom-call | tf_op jit(solution)/shard_map/splat_views/pallas_call | solution.py:440
  47.9 1.7 %write_outputs.1 = (bf16[2,2,128,256]{3,2,1,0:T(8,128)(2,1)}, bf16[1,256,128]{2,1,0:T(8,128)(2,1)}, f32[1,256]{1,0:T(1,128)}, f32[2,5,1,256]{3,2,1,0:T(1,128)}) custom-call(bf16[2,2,128,256]{3,2,1,0:T(8,128)(2,1)} %get-tuple-element.12.img_ref, bf16[256,128]{1,0:T(8,128)(2,1)} %get-tuple-element.13.newf_ref, f32[1,256]{1,0:T(1,128)} %get-tuple-element.14.newl_ref, ...), custom_call_target="tpu_custom_call" | custom-call | tf_op jit(solution)/shard_map/write_outputs/pallas_call | solution.py:505

commit v5 on v4

--- a/solution.py
+++ b/solution.py
@@ -381,11 +381,11 @@
                 copy.start()
 
         steps(1, layers, bwd_step)
+        image_copy(v).start()
         backward(v, me_d, in_f, in_s)
         for k in range(1, layers):
             for copy in give(k):
                 copy.wait()
-        image_copy(v).start()
         sums_f = []
         sums_s = []
         for t in range(tiles):

time: 49.8 us -> 51.6 us (1.036)
  Pallas kernels: 49 us -> 50.7 us
    pallas_call x1, Pallas kernels: 47.2 us -> 49 us  [body(): pl.pallas_call(functools.partial(splat_kernel, owners, layers, views, til...]
where the time goes in v5:
time: 51.6 us; the launch traced here: 51.4 us
  Pallas kernels  50.7 us (98%)
  between operations  0.64 us (1%)
    pallas_call x1, Pallas kernels, body(): pl.pallas_call(functools.partial(splat_kernel, owners, layers, views, til...  49 us
    pallas_call x1, Pallas kernels, body(): pl.pallas_call(finish_kernel, out_shape=(jax.ShapeDtypeStruct(images.shap...  1.73 us

profile of v5, /device:TPU:0, one launch (start us, length us, event | category | flops | bytes accessed | tf_op | source)
XLA Modules:
  0.0 51.4 jit_solution(889054395667179380)
XLA Ops:
  0.6 49.0 %splat_views.1 = (bf16[2,2,128,256]{3,2,1,0:T(8,128)(2,1)}, bf16[256,128]{1,0:T(8,128)(2,1)}, f32[1,256]{1,0:T(1,128)}, f32[2,8,256]{2,1,0:T(8,128)}) custom-call(bf16[256,128]{1,0:T(8,128)(2,1)} %bitcast.3, f32[1,256]{1,0:T(1,128)} %logit_ref.1, f32[2,5,1,256]{3,2,1,0:T(1,128)} %bitcast.4, s32[2,1,256]{2,1,0:T(1,128)} %dest_ref.1, ...), custom_call_target="tpu_custom_call" | custom-call | tf_op jit(solution)/shard_map/splat_views/pallas_call | solution.py:440
  49.6 1.7 %write_outputs.1 = (bf16[2,2,128,256]{3,2,1,0:T(8,128)(2,1)}, bf16[1,256,128]{2,1,0:T(8,128)(2,1)}, f32[1,256]{1,0:T(1,128)}, f32[2,5,1,256]{3,2,1,0:T(1,128)}) custom-call(bf16[2,2,128,256]{3,2,1,0:T(8,128)(2,1)} %get-tuple-element.12.img_ref, bf16[256,128]{1,0:T(8,128)(2,1)} %get-tuple-element.13.newf_ref, f32[1,256]{1,0:T(1,128)} %get-tuple-element.14.newl_ref, ...), custom_call_target="tpu_custom_call" | custom-call | tf_op jit(solution)/shard_map/write_outputs/pallas_call | solution.py:505
